TPU v7x, 32 devices: a whole 2x2x4 slice. The times are simulated.
32 devices in a mesh: row: 8 (over z, y), col: 4 (over x, core).
Axes of the slice: x: 2, y: 2, z: 4, core: 2. Of those that a mesh axis runs over, the one named last changes fastest.
Arguments:
- contact_map: float32 [256, 256], P('row', 'col'), may hold values from -6 to 6
- embed_weight: bfloat16 [16, 128], replicated, may hold values from -1.5 to 1.5
- embed_bias: float32 [128], replicated, may hold values from -3 to 3
- conv_weight: bfloat16 [3, 3, 3, 128, 128], replicated, may hold values from -0.1875 to 0.1875
- conv_bias: float32 [3, 128], replicated, may hold values from -3 to 3
- mix_weight: bfloat16 [128, 128], replicated, may hold values from -0.5 to 0.5
- mix_bias: float32 [128], replicated, may hold values from -6 to 6
- proj_weight: bfloat16 [128, 256], replicated, may hold values from -1 to 1
- proj_bias: float32 [256], replicated, may hold values from -3 to 3
- up_weight: bfloat16 [256, 1024], replicated, may hold values from -0.375 to 0.375
- up_bias: float32 [1024], replicated, may hold values from -3 to 3
- down_weight: bfloat16 [1024, 256], replicated, may hold values from -0.1875 to 0.1875
- down_bias: float32 [256], replicated, may hold values from -3 to 3
Outputs:
- latents: bfloat16 [64, 256], P(('row', 'col'))
- sym: bfloat16 [64, 64, 128], P('row', 'col')
All inputs are finite; a program needn't handle non-finite values.
Results may differ from a plain program's by a relative error of at most 0.0085.
Values may be sent and summed in bfloat16 or wider, within the bound.
No kernel may reach another device: no remote copies, remote signals or barrier semaphores. Data moves between devices by JAX's collectives and lax.ppermute only.
A program may use at most 64 MiB of HBM per device.

v0:
```python
import jax
import jax.numpy as jnp
from jax import lax
from jax.sharding import PartitionSpec as P

PATCH = 4
LAYERS = 3


def with_halo(array, sides, width):
    for axis, dim in sides:
        count, length = (lax.axis_size(axis), array.shape[dim])
        up = [(i, (i + 1) % count) for i in range(count - 1)]
        down = [(j, i) for i, j in up]
        last = lax.slice_in_dim(array, length - width, length, axis=dim)
        initial = lax.slice_in_dim(array, 0, width, axis=dim)
        before = lax.ppermute(last, axis, up)
        after = lax.ppermute(initial, axis, down)
        array = jnp.concatenate([before, array, after], axis=dim)
    return array


def conv_layer(padded, weight, bias, rows, cols):
    width = padded.shape[2]
    total = jnp.zeros((rows * cols, weight.shape[3]), jnp.float32)
    for offset_a in range(3):
        for offset_b in range(3):
            window = padded[offset_a : offset_a + rows, offset_b : offset_b + cols].reshape(
                rows * cols, width
            )
            total = total + jnp.dot(
                window, weight[offset_a, offset_b], preferred_element_type=jnp.float32
            )
    return jax.nn.gelu(total + bias).reshape(rows, cols, weight.shape[3])


def mirror_strips(feat, count_row, count_col, total_cells):
    width = feat.shape[2]
    strip = lax.all_to_all(feat, "col", split_axis=0, concat_axis=1, tiled=True)
    unit = strip.shape[0]
    blocks = strip.reshape(unit, count_row, count_col, unit, width)
    moved = lax.all_to_all(
        lax.all_to_all(blocks, "row", split_axis=1, concat_axis=1, tiled=True),
        "col",
        split_axis=2,
        concat_axis=2,
        tiled=True,
    )
    mirrored = moved.transpose(3, 1, 2, 0, 4).reshape(unit, total_cells, width)
    return (strip, mirrored)


def back_to_tiles(strip_values):
    return lax.all_to_all(strip_values, "col", split_axis=1, concat_axis=0, tiled=True)


def average_pair(first, second):
    return ((first.astype(jnp.float32) + second.astype(jnp.float32)) * 0.5).astype(jnp.bfloat16)


def mixed_sums(sym, mix_weight, mix_bias):
    lead, span, width = sym.shape
    mixed = jax.nn.gelu(
        jnp.dot(sym.reshape(lead * span, width), mix_weight, preferred_element_type=jnp.float32)
        + mix_bias
    )
    return jnp.sum(mixed.reshape(lead, span, width), axis=1)


def tile_pool(sym, mix_weight, mix_bias):
    partial_value = mixed_sums(sym, mix_weight, mix_bias)
    return lax.psum_scatter(partial_value, "col", scatter_dimension=0, tiled=True)


def tiles_path(feat, count_row, count_col, total_cells, mix_weight, mix_bias):
    strip, mirrored = mirror_strips(feat, count_row, count_col, total_cells)
    returned = back_to_tiles(mirrored)
    sym = average_pair(feat, returned)
    return (tile_pool(sym, mix_weight, mix_bias), sym)


def body(
    contact_map,
    embed_weight,
    embed_bias,
    conv_weight,
    conv_bias,
    mix_weight,
    mix_bias,
    proj_weight,
    proj_bias,
    up_weight,
    up_bias,
    down_weight,
    down_bias,
):
    tile_rows = contact_map.shape[0] // PATCH
    tile_cols = contact_map.shape[1] // PATCH
    width = embed_weight.shape[1]
    grid = contact_map.reshape(tile_rows, PATCH, tile_cols, PATCH).transpose(0, 2, 1, 3)
    patches = grid.reshape(tile_rows * tile_cols, PATCH * PATCH).astype(jnp.bfloat16)
    embedded = jnp.dot(patches, embed_weight, preferred_element_type=jnp.float32) + embed_bias
    feat = embedded.astype(jnp.bfloat16).reshape(tile_rows, tile_cols, width)
    count_row = lax.axis_size("row")
    count_col = lax.axis_size("col")
    total_cells = tile_rows * count_row
    depth = LAYERS
    padded = with_halo(feat, (("row", 0), ("col", 1)), depth)
    row_anchor = lax.axis_index("row") * tile_rows - depth
    col_anchor = lax.axis_index("col") * tile_cols - depth
    current = padded
    for layer in range(LAYERS):
        margin = depth - layer - 1
        rows = tile_rows + 2 * margin
        cols = tile_cols + 2 * margin
        output = conv_layer(current, conv_weight[layer], conv_bias[layer], rows, cols).astype(
            jnp.bfloat16
        )
        if margin > 0:
            row_global = row_anchor + layer + 1 + jnp.arange(rows, dtype=jnp.int32)
            col_global = col_anchor + layer + 1 + jnp.arange(cols, dtype=jnp.int32)
            row_inside = (row_global >= 0) & (row_global < total_cells)
            col_inside = (col_global >= 0) & (col_global < total_cells)
            inside = row_inside[:, None] & col_inside[None, :]
            output = jnp.where(inside[:, :, None], output, jnp.zeros((), jnp.bfloat16))
        current = output
    feat = current
    summed, sym_tile = tiles_path(feat, count_row, count_col, total_cells, mix_weight, mix_bias)
    pooled = (summed / total_cells).astype(jnp.bfloat16)
    latent = jnp.dot(pooled, proj_weight, preferred_element_type=jnp.float32) + proj_bias
    hidden = jax.nn.gelu(
        jnp.dot(latent.astype(jnp.bfloat16), up_weight, preferred_element_type=jnp.float32)
        + up_bias
    ).astype(jnp.bfloat16)
    result = latent + jnp.dot(hidden, down_weight, preferred_element_type=jnp.float32) + down_bias
    return (result.astype(jnp.bfloat16), sym_tile)


def solution(mesh):
    return jax.shard_map(
        body,
        mesh=mesh,
        in_specs=(P("row", "col"), P(), P(), P(), P(), P(), P(), P(), P(), P(), P(), P(), P()),
        out_specs=(P(("row", "col"), None), P("row", "col", None)),
        check_vma=False,
    )
```

profile of v0, /device:TPU:0, one launch (start us, length us, event | category | flops | bytes accessed | tf_op | source)
XLA Modules:
  0.0 67.8 jit_solution(5237650982164212226)
XLA Ops:
  0.6 0.8 %convert_element_type.78 = bf16[32,64]{1,0:T(8,128)(2,1)S(1)} convert(f32[32,64]{1,0:T(8,128)} %param.13) | non-fusion elementwise | flops 2048 | bytes 12288 | tf_op jit(solution)/shard_map/convert_element_type | solution.py:101
  1.4 0.2 convert_element_type.79
  1.6 0.3 copy.23
  2.0 0.6 copy-done.4
  2.6 0.2 fusion.3
  2.8 1.3 %collective-permute-start.1 = (bf16[3,16,128]{2,1,0:T(8,128)(2,1)S(1)}, bf16[3,16,128]{2,1,0:T(8,128)(2,1)S(1)}, u32[]{:S(2)}, u32[]{:S(2)}) collective-permute-start(bf16[3,16,128]{2,1,0:T(8,128)(2,1)S(1)} %bitcast.190), channel_id=1, source_target_pairs={{4,0},{8,4},{12,8},{16,12},{20,16},{24,20},{28,24},{5,1},{9,5},{13... | collective-permute-start | bytes 36872 | tf_op jit(solution)/shard_map/ppermute | solution.py:18
  4.1 5.5 %collective-permute-start = (bf16[3,16,128]{2,1,0:T(8,128)(2,1)S(1)}, bf16[3,16,128]{2,1,0:T(8,128)(2,1)S(1)}, u32[]{:S(2)}, u32[]{:S(2)}) collective-permute-start(bf16[3,16,128]{2,1,0:T(8,128)(2,1)S(1)} %bitcast.189), channel_id=1, source_target_pairs={{0,4},{4,8},{8,12},{12,16},{16,20},{20,24},{24,28},{1,5},{5,9},{9,... | collective-permute-start | bytes 36872 | tf_op jit(solution)/shard_map/ppermute | solution.py:17
  9.7 0.6 copy-done.5
  10.3 1.2 %slice_bitcast_fusion = (bf16[3,3,128,128]{3,2,1,0:T(8,128)(2,1)S(1)}, bf16[3,3,128,128]{3,2,1,0:T(8,128)(2,1)S(1)}, bf16[3,3,128,128]{3,2,1,0:T(8,128)(2,1)S(1)}) fusion(bf16[3,3,3,128,128]{4,3,2,1,0:T(8,128)(2,1)} %param.16), kind=kLoop, calls=%fused_computation.35 | loop fusion | bytes 1769472 | tf_op jit(solution)/shard_map/squeeze | solution.py:116
  11.7 1.5 %collective-permute-start.2 = (bf16[14,3,128]{2,1,0:T(4,128)(2,1)S(1)}, bf16[14,3,128]{2,1,0:T(4,128)(2,1)S(1)}, u32[]{:S(2)}, u32[]{:S(2)}) collective-permute-start(bf16[14,3,128]{2,1,0:T(4,128)(2,1)S(1)} %get-tuple-element.32), channel_id=1, source_target_pairs={{0,1},{1,2},{2,3},{4,5},{5,6},{6,7},{8,9},{9,10},{10,11},{12,13},{... | collective-permute-start | bytes 32264 | tf_op jit(solution)/shard_map/ppermute | solution.py:17
  13.1 1.3 %collective-permute-start.3 = (bf16[14,3,128]{2,1,0:T(4,128)(2,1)S(1)}, bf16[14,3,128]{2,1,0:T(4,128)(2,1)S(1)}, u32[]{:S(2)}, u32[]{:S(2)}) collective-permute-start(bf16[14,3,128]{2,1,0:T(4,128)(2,1)S(1)} %get-tuple-element.33), channel_id=1, source_target_pairs={{1,0},{2,1},{3,2},{5,4},{6,5},{7,6},{9,8},{10,9},{11,10},{13,12},{... | collective-permute-start | bytes 32264 | tf_op jit(solution)/shard_map/ppermute | solution.py:18
  14.5 3.7 %collective-permute-done.3 = bf16[14,3,128]{2,1,0:T(4,128)(2,1)S(1)} collective-permute-done((bf16[14,3,128]{2,1,0:T(4,128)(2,1)S(1)}, bf16[14,3,128]{2,1,0:T(4,128)(2,1)S(1)}, u32[]{:S(2)}, u32[]{:S(2)}) %collective-permute-start.3) | collective-permute-done | bytes 10784 | tf_op jit(solution)/shard_map/ppermute | solution.py:18
  18.8 0.2 convolution_add_fusion.7
  19.3 0.2 convolution_add_fusion.4
  19.9 0.2 convolution_add_fusion.1
  20.0 0.2 fusion.13
  20.9 0.2 convolution_add_fusion.15
  21.7 0.2 convolution_add_fusion.10
  22.1 0.2 fusion.21
  23.6 0.2 fusion.29
  23.8 7.5 %all_to_all.34 = bf16[8,16,128]{2,1,0:T(8,128)(2,1)S(1)} all-to-all(bf16[8,16,128]{2,1,0:T(8,128)(2,1)S(1)} %bitcast.173), channel_id=1, replica_groups=mesh['row'=8,'col'=4] {'col'}, dimensions={0} | all-to-all | bytes 65536 | tf_op jit(solution)/shard_map/all_to_all | solution.py:39
  31.3 13.3 %all_to_all.35 = bf16[2,8,4,2,128]{4,3,2,0,1:T(2,128)(2,1)S(1)} all-to-all(bf16[2,8,4,2,128]{4,3,2,0,1:T(2,128)(2,1)S(1)} %copy.25), channel_id=1, replica_groups=mesh['row'=8,'col'=4] {'row'}, dimensions={1} | all-to-all | bytes 65536 | tf_op jit(solution)/shard_map/all_to_all | solution.py:43
  44.6 6.3 %all_to_all.36 = bf16[2,8,4,2,128]{4,3,1,0,2:T(2,128)(2,1)S(1)} all-to-all(bf16[2,8,4,2,128]{4,3,1,0,2:T(2,128)(2,1)S(1)} %copy.26), channel_id=1, replica_groups=mesh['row'=8,'col'=4] {'col'}, dimensions={2} | all-to-all | bytes 65536 | tf_op jit(solution)/shard_map/all_to_all | solution.py:42
  50.9 0.6 copy.28
  51.6 3.3 %all-to-all-start.3 = ((bf16[2,64,128]{2,0,1:T(2,128)(2,1)}), bf16[2,64,128]{2,0,1:T(2,128)(2,1)S(1)}, u32[]{:S(2)}, u32[]{:S(2)}) async-start(bf16[2,64,128]{2,0,1:T(2,128)(2,1)} %copy.28), calls=%async_computation.3 | async-start | bytes 65536 | tf_op jit(solution)/shard_map/all_to_all | solution.py:54
  54.9 0.6 dynamic-slice
  56.1 2.7 %all-to-all-done.3 = bf16[2,64,128]{2,0,1:T(2,128)(2,1)S(1)} async-done(((bf16[2,64,128]{2,0,1:T(2,128)(2,1)}), bf16[2,64,128]{2,0,1:T(2,128)(2,1)S(1)}, u32[]{:S(2)}, u32[]{:S(2)}) %all-to-all-start.3) | async-done | bytes 32800 | tf_op jit(solution)/shard_map/all_to_all | solution.py:54
  58.8 0.6 fusion.38
  59.4 0.7 %copy-done.9 = bf16[128,128]{1,0:T(8,128)(2,1)S(1)} copy-done((bf16[128,128]{1,0:T(8,128)(2,1)S(1)}, bf16[128,128]{1,0:T(8,128)(2,1)}, u32[]{:S(2)}) %copy-start.9) | copy-done | bytes 32792
  60.4 5.8 %all-reduce = f32[8,128]{1,0:T(8,128)S(1)} all-reduce(f32[8,128]{1,0:T(8,128)S(1)} %bitcast_reduce_fusion), channel_id=2, replica_groups=mesh['row'=8,'col'=4] {'col'}, use_global_device_ids=true, to_apply=%region_1.2.clone | all-reduce | flops 1024 | bytes 8192
  66.3 0.5 copy-done.3
  66.8 0.9 %fusion.5 = bf16[2,256]{1,0:T(2,128)(2,1)} fusion(f32[2,256]{1,0:T(2,128)S(1)} %convolution_add_fusion.27, bf16[1024,256]{1,0:T(8,128)(2,1)S(1)} %copy-done, bf16[256,1024]{1,0:T(8,128)(2,1)S(1)} %copy-done.1, f32[1024]{0:T(1024)S(1)} %copy-done.3, f32[256]{0:T(256)S(1)} %copy-done.7), kind=kOutput, calls=%fused_computation.34 | convolution fusion | flops 2119680 | bytes 1056768 | tf_op jit(solution)/shard_map/dot_general | solution.py:135
  (88 shorter events, 4.5 us)
Async XLA Ops:
  0.6 65.7 %copy-start = (bf16[1024,256]{1,0:T(8,128)(2,1)S(1)}, bf16[1024,256]{1,0:T(8,128)(2,1)}, u32[]{:S(2)}) copy-start(bf16[1024,256]{1,0:T(8,128)(2,1)} %param.24) | copy-start | bytes 1572868
  1.9 0.7 %copy-start.4 = (bf16[16,128]{1,0:T(8,128)(2,1)S(1)}, bf16[16,128]{1,0:T(8,128)(2,1)}, u32[]{:S(2)}) copy-start(bf16[16,128]{1,0:T(8,128)(2,1)} %param.14) | copy-start | bytes 12292
  1.9 0.7 %copy-start.8 = (f32[128]{0:T(128)S(1)}, f32[128]{0:T(128)}, u32[]{:S(2)}) copy-start(f32[128]{0:T(128)} %param.15) | copy-start | bytes 1540
  2.8 8.8 %collective-permute-start.1 = (bf16[3,16,128]{2,1,0:T(8,128)(2,1)S(1)}, bf16[3,16,128]{2,1,0:T(8,128)(2,1)S(1)}, u32[]{:S(2)}, u32[]{:S(2)}) collective-permute-start(bf16[3,16,128]{2,1,0:T(8,128)(2,1)S(1)} %bitcast.190), channel_id=1, source_target_pairs={{4,0},{8,4},{12,8},{16,12},{20,16},{24,20},{28,24},{5,1},{9,5},{13... | collective-permute-start | bytes 36872 | tf_op jit(solution)/shard_map/ppermute | solution.py:18
  4.1 7.5 %collective-permute-start = (bf16[3,16,128]{2,1,0:T(8,128)(2,1)S(1)}, bf16[3,16,128]{2,1,0:T(8,128)(2,1)S(1)}, u32[]{:S(2)}, u32[]{:S(2)}) collective-permute-start(bf16[3,16,128]{2,1,0:T(8,128)(2,1)S(1)} %bitcast.189), channel_id=1, source_target_pairs={{0,4},{4,8},{8,12},{12,16},{16,20},{20,24},{24,28},{1,5},{5,9},{9,... | collective-permute-start | bytes 36872 | tf_op jit(solution)/shard_map/ppermute | solution.py:17
  9.7 0.7 %copy-start.5 = (f32[3,128]{1,0:T(4,128)S(1)}, f32[3,128]{1,0:T(4,128)}, u32[]{:S(2)}) copy-start(f32[3,128]{1,0:T(4,128)} %param.17) | copy-start | bytes 4612
  11.7 2.8 %collective-permute-start.2 = (bf16[14,3,128]{2,1,0:T(4,128)(2,1)S(1)}, bf16[14,3,128]{2,1,0:T(4,128)(2,1)S(1)}, u32[]{:S(2)}, u32[]{:S(2)}) collective-permute-start(bf16[14,3,128]{2,1,0:T(4,128)(2,1)S(1)} %get-tuple-element.32), channel_id=1, source_target_pairs={{0,1},{1,2},{2,3},{4,5},{5,6},{6,7},{8,9},{9,10},{10,11},{12,13},{... | collective-permute-start | bytes 32264 | tf_op jit(solution)/shard_map/ppermute | solution.py:17
  13.1 5.1 %collective-permute-start.3 = (bf16[14,3,128]{2,1,0:T(4,128)(2,1)S(1)}, bf16[14,3,128]{2,1,0:T(4,128)(2,1)S(1)}, u32[]{:S(2)}, u32[]{:S(2)}) collective-permute-start(bf16[14,3,128]{2,1,0:T(4,128)(2,1)S(1)} %get-tuple-element.33), channel_id=1, source_target_pairs={{1,0},{2,1},{3,2},{5,4},{6,5},{7,6},{9,8},{10,9},{11,10},{13,12},{... | collective-permute-start | bytes 32264 | tf_op jit(solution)/shard_map/ppermute | solution.py:18
  31.3 23.6 %copy-start.11 = (u32[32]{0:T(128)S(1)}, u32[32]{0:T(128)}, u32[]{:S(2)}) copy-start(u32[32]{0:T(128)} %constant.14) | copy-start | bytes 388
  50.9 15.4 %copy-start.1 = (bf16[256,1024]{1,0:T(8,128)(2,1)S(1)}, bf16[256,1024]{1,0:T(8,128)(2,1)}, u32[]{:S(2)}) copy-start(bf16[256,1024]{1,0:T(8,128)(2,1)} %param.22) | copy-start | bytes 1572868
  51.6 7.2 %all-to-all-start.3 = ((bf16[2,64,128]{2,0,1:T(2,128)(2,1)}), bf16[2,64,128]{2,0,1:T(2,128)(2,1)S(1)}, u32[]{:S(2)}, u32[]{:S(2)}) async-start(bf16[2,64,128]{2,0,1:T(2,128)(2,1)} %copy.28), calls=%async_computation.3 | async-start | bytes 65536 | tf_op jit(solution)/shard_map/all_to_all | solution.py:54
  59.4 0.8 %copy-start.9 = (bf16[128,128]{1,0:T(8,128)(2,1)S(1)}, bf16[128,128]{1,0:T(8,128)(2,1)}, u32[]{:S(2)}) copy-start(bf16[128,128]{1,0:T(8,128)(2,1)} %param.18) | copy-start | bytes 98308
  59.4 0.8 %copy-start.10 = (f32[128]{0:T(128)S(1)}, f32[128]{0:T(128)}, u32[]{:S(2)}) copy-start(f32[128]{0:T(128)} %param.19) | copy-start | bytes 1540
  60.2 6.0 %copy-start.2 = (bf16[128,256]{1,0:T(8,128)(2,1)S(1)}, bf16[128,256]{1,0:T(8,128)(2,1)}, u32[]{:S(2)}) copy-start(bf16[128,256]{1,0:T(8,128)(2,1)} %param.20) | copy-start | bytes 196612
  60.4 5.8 %copy-start.6 = (f32[256]{0:T(256)S(1)}, f32[256]{0:T(256)}, u32[]{:S(2)}) copy-start(f32[256]{0:T(256)} %param.21) | copy-start | bytes 3076
  66.1 0.7 %copy-start.3 = (f32[1024]{0:T(1024)S(1)}, f32[1024]{0:T(1024)}, u32[]{:S(2)}) copy-start(f32[1024]{0:T(1024)} %param.23) | copy-start | bytes 12292
  66.2 0.7 %copy-start.7 = (f32[256]{0:T(256)S(1)}, f32[256]{0:T(256)}, u32[]{:S(2)}) copy-start(f32[256]{0:T(256)} %param.25) | copy-start | bytes 3076
where the time goes:
time: 68.4 us; the launch traced here: 67.8 us
  blocking collectives  32.8 us (48%)
  starting transfers between devices  12.8 us (19%)
  waiting for transfers between devices  6.41 us (9%)
  local copies, waits for them, and re-layouts  6.24 us (9%)
  matrix products  5.73 us (8%)
  other arithmetic  1.88 us (3%)
  between operations  1.85 us (3%)
    all_to_all x1, blocking collectives, mirror_strips(): lax.all_to_all(blocks, 'row', split_axis=1, concat_axis=1, tiled=True)  13.3 us
    all_to_all x1, blocking collectives, mirror_strips(): strip = lax.all_to_all(feat, 'col', split_axis=0, concat_axis=1, tiled=True)  7.47 us
    ppermute x2, starting transfers between devices, with_halo(): before = lax.ppermute(last, axis, up)  6.99 us
    all_to_all x1, blocking collectives, mirror_strips(): lax.all_to_all(lax.all_to_all(blocks, 'row', split_axis=1, concat_axis=1,...  6.3 us
    unnamed x1, blocking collectives  5.77 us
    dot_general x27, matrix products, conv_layer(): jnp.dot(window, weight[offset_a, offset_b], preferred_element_type=jnp.fl...  4.3 us
    ppermute x2, waiting for transfers between devices, with_halo(): after = lax.ppermute(initial, axis, down)  3.75 us
    all_to_all x1, starting transfers between devices, back_to_tiles(): lax.all_to_all(strip_values, 'col', split_axis=1, concat_axis=0, tiled=True)  3.26 us
  transfers between devices with their start and end apart: 5, of which 2 were waited for; matrix products, arithmetic and copies ran while one was open for 3% of the time, Pallas kernels for 0%

commit v1 on v0

v1 whole, which is shorter than its diff:
```python
import functools

import jax
import jax.numpy as jnp
from jax import lax
from jax.experimental import pallas as pl
from jax.experimental.pallas import tpu as pltpu
from jax.sharding import PartitionSpec as P

PATCH = 4
LAYERS = 3
UNROLL_CELLS = 2048
CHUNK_CELLS = 256


def gelu(x):
    scale = 0.7978845608028654
    half = 0.5 * x
    return half + half * jnp.tanh(x * (scale + (scale * 0.044715) * (x * x)))


def for_rows(total, span, step):
    if total * span <= UNROLL_CELLS:
        chunk = max(1, CHUNK_CELLS // span)
        for start in range(0, total, chunk):
            step(start, min(chunk, total - start))
    else:
        lax.fori_loop(0, total, lambda r, carry: (step(r, 1), carry)[1], 0)


def encoder_kernel(
    gathered, embed_w, embed_b, conv_w, conv_b, mix_w, mix_b, proj_w, proj_b,
    up_w, up_b, down_w, down_b, latents, sym_out, *buffers, tile_rows, tile_cols, shared,
):
    n_row, n_col, pixels, cells = gathered.shape
    width = embed_w.shape[1]
    span = n_row * tile_rows
    own_rows = latents.shape[0]
    row = lax.axis_index("row")
    col = lax.axis_index("col")
    origin = row * tile_rows - LAYERS

    def keep_inside(value, first):
        rows = first + lax.broadcasted_iota(jnp.int32, value.shape, 0)
        return jnp.where((rows >= 0) & (rows < span), value, 0.0)

    def emit(target, start, value):
        count = value.shape[0]
        place = lax.broadcasted_iota(jnp.int32, value.shape, 1)
        left = jnp.where(place == 0, 0.0, pltpu.roll(value, 1, 1))
        right = jnp.where(place == span - 1, 0.0, pltpu.roll(value, span - 1, 1))
        for at, part in enumerate((left, value, right)):
            target[pl.ds(start, count), :, at * width : (at + 1) * width] = part.astype(jnp.bfloat16)

    def block_weight(group):
        tiled = jnp.concatenate([embed_w[...].astype(jnp.float32)] * group, axis=0)
        tiled = jnp.concatenate([tiled] * group, axis=1)
        at_row = lax.broadcasted_iota(jnp.int32, tiled.shape, 0) // pixels
        at_col = lax.broadcasted_iota(jnp.int32, tiled.shape, 1) // width
        return jnp.where(at_row == at_col, tiled, 0.0).astype(jnp.bfloat16)

    def embed(target, flipped):
        group, inner = (n_row, tile_rows) if flipped else (n_col, tile_cols)
        weight = block_weight(group)
        bias = embed_b[...].reshape(1, width)
        bias = jnp.concatenate([bias] * group, axis=1)
        if flipped:
            first_tile = (origin + tile_cols) // tile_cols - 1
            firsts = [r * tile_rows - LAYERS for r in range(n_row)]
            count = max(
                (f + tile_rows + 2 * LAYERS - 1) // tile_cols - f // tile_cols + 1 for f in firsts
            )
            tiles = [first_tile + t for t in range(count)]
            limit = n_col - 1
            outer = tile_cols
        else:
            tiles = [row - 1, row, row + 1]
            limit = n_row - 1
            outer = tile_rows

        def step(start, rows):
            shape = (rows, inner, cells)
            major = lax.broadcasted_iota(jnp.int32, shape, 0) + start + origin
            minor = lax.broadcasted_iota(jnp.int32, shape, 1)
            lane = lax.broadcasted_iota(jnp.int32, shape, 2)
            picked = None
            for tile in tiles:
                offset = major - tile * outer
                ok = (offset >= 0) & (offset < outer)
                goal = minor * tile_cols + offset if flipped else offset * tile_cols + minor
                select = jnp.where(ok & (lane == goal), 1.0, 0.0)
                select = select.reshape(rows * inner, cells).astype(jnp.bfloat16)
                at = jnp.clip(tile, 0, limit)
                source = gathered[:, at] if flipped else gathered[at]
                source = source.reshape(group * pixels, cells)
                part = lax.dot_general(
                    select, source, (((1,), (1,)), ((), ())), preferred_element_type=jnp.float32
                )
                picked = part if picked is None else picked + part
            value = jnp.dot(picked.astype(jnp.bfloat16), weight, preferred_element_type=jnp.float32)
            value = value + bias
            value = jnp.concatenate(
                [
                    value[:, g * width : (g + 1) * width].reshape(rows, inner, width)
                    for g in range(group)
                ],
                axis=1,
            )
            emit(target, start, keep_inside(value, start + origin))

        for_rows(tile_rows + 2 * LAYERS, span, step)

    def taps(layer, flipped):
        if flipped:
            return [conv_w[layer, :, a].reshape(3 * width, width) for a in range(3)]
        return [conv_w[layer, a].reshape(3 * width, width) for a in range(3)]

    def convolve(source, layer, flipped, start, rows, place, extent):
        total = conv_b[layer : layer + 1, :]
        for a, weight in enumerate(taps(layer, flipped)):
            window = source[pl.ds(start + a, rows), pl.ds(place, extent), :]
            window = window.reshape(rows * extent, 3 * width)
            total = total + jnp.dot(window, weight, preferred_element_type=jnp.float32)
        return gelu(total).reshape(rows, extent, width)

    def features(flipped, first, second, third):
        embed(first, flipped)
        for layer, source, target in ((0, first, second), (1, second, third)):

            def step(start, rows, layer=layer, source=source, target=target):
                value = convolve(source, layer, flipped, start, rows, 0, span)
                emit(target, start, keep_inside(value, start + origin + layer + 1))

            for_rows(tile_rows + 2 * (LAYERS - layer - 1), span, step)
        place = pl.multiple_of(col * tile_cols, tile_cols)
        tile = convolve(third, LAYERS - 1, flipped, 0, tile_rows, place, tile_cols)
        strip = convolve(third, LAYERS - 1, flipped, col * own_rows, own_rows, 0, span)
        return tile.astype(jnp.bfloat16), strip.astype(jnp.bfloat16)

    def average(first, second):
        total = first.astype(jnp.float32) + second.astype(jnp.float32)
        return (total * 0.5).astype(jnp.bfloat16)

    one, two, three = buffers[:3]
    tile, strip = features(False, one, two, three)
    if shared:
        four, five, six = one, two, three
    else:
        four, five, six = buffers[3:6]
    flipped_tile, flipped_strip = features(True, four, five, six)
    sym_out[...] = average(tile, flipped_tile)
    sym = average(strip, flipped_strip).reshape(own_rows * span, width)
    mixed = jnp.dot(sym, mix_w[...], preferred_element_type=jnp.float32) + mix_b[...].reshape(1, width)
    summed = jnp.sum(gelu(mixed).reshape(own_rows, span, width), axis=1)
    pooled = (summed / span).astype(jnp.bfloat16)
    latent = jnp.dot(pooled, proj_w[...], preferred_element_type=jnp.float32)
    latent = latent + proj_b[...].reshape(1, -1)
    hidden = jnp.dot(latent.astype(jnp.bfloat16), up_w[...], preferred_element_type=jnp.float32)
    hidden = gelu(hidden + up_b[...].reshape(1, -1)).astype(jnp.bfloat16)
    result = jnp.dot(hidden, down_w[...], preferred_element_type=jnp.float32)
    latents[...] = (latent + result + down_b[...].reshape(1, -1)).astype(jnp.bfloat16)


def body(contact_map, embed_weight, *rest):
    n_row, n_col = lax.axis_size("row"), lax.axis_size("col")
    tile_rows = contact_map.shape[0] // PATCH
    tile_cols = contact_map.shape[1] // PATCH
    pixels, width = embed_weight.shape
    cells = tile_rows * tile_cols
    grid = contact_map.astype(jnp.bfloat16).reshape(tile_rows, PATCH, tile_cols, PATCH)
    patches = grid.transpose(1, 3, 0, 2).reshape(1, pixels, cells)
    sent = jnp.broadcast_to(patches, (n_row * n_col, pixels, cells))
    gathered = lax.all_to_all(sent, ("row", "col"), 0, 0, tiled=True)
    gathered = gathered.reshape(n_row, n_col, pixels, cells)
    span = n_row * tile_rows
    own_rows = tile_rows // n_col
    out_width = rest[-1].shape[0]
    heights = [tile_rows + 2 * (LAYERS - layer) for layer in range(LAYERS)]
    buffers = [pltpu.VMEM((h, span, 3 * width), jnp.bfloat16) for h in heights]
    shared = sum(heights) * span > UNROLL_CELLS * 2
    if not shared:
        buffers = buffers * 2
    whole = pl.BlockSpec(memory_space=pltpu.VMEM)
    kernel = functools.partial(
        encoder_kernel, tile_rows=tile_rows, tile_cols=tile_cols, shared=shared
    )
    return pl.pallas_call(
        kernel,
        out_shape=(
            jax.ShapeDtypeStruct((own_rows, out_width), jnp.bfloat16),
            jax.ShapeDtypeStruct((tile_rows, tile_cols, width), jnp.bfloat16),
        ),
        in_specs=[whole] * (2 + len(rest)),
        out_specs=(whole, whole),
        scratch_shapes=buffers,
        name="encoder",
    )(gathered, embed_weight, *rest)


def solution(mesh):
    return jax.shard_map(
        body,
        mesh=mesh,
        in_specs=(P("row", "col"), P(), P(), P(), P(), P(), P(), P(), P(), P(), P(), P(), P()),
        out_specs=(P(("row", "col"), None), P("row", "col", None)),
        check_vma=False,
    )
```

time: 68.4 us -> 24.6 us (0.36)
  blocking collectives: 32.8 us -> 15.4 us
  starting transfers between devices: 12.8 us -> 0 us
  Pallas kernels: 0 us -> 6.92 us
  waiting for transfers between devices: 6.41 us -> 0 us
  matrix products: 5.73 us -> 0 us
  local copies, waits for them, and re-layouts: 6.24 us -> 0.59 us
  between operations: 1.85 us -> 0.65 us
  other arithmetic: 1.88 us -> 0.72 us
    all_to_all x3 -> x1, blocking collectives: 27.1 us -> 15.4 us  [body(): gathered = lax.all_to_all(sent, ('row', 'col'), 0, 0, tiled=True)]
    ppermute x4 -> x0, starting transfers between devices: 9.57 us -> none  [the longest x2 6.99 us: with_halo(): before = lax.ppermute(last, axis, up)]
    pallas_call x0 -> x1, Pallas kernels: none -> 6.92 us  [body(): pl.pallas_call(kernel, out_shape=(jax.ShapeDtypeStruct((own_rows, out_wid...]
    unnamed x1 -> x0, blocking collectives: 5.77 us -> none
    dot_general x31 -> x0, matrix products: 5.73 us -> none  [the longest x27 4.3 us: conv_layer(): jnp.dot(window, weight[offset_a, offset_b], preferred_element_type=jnp.fl...]
    ppermute x4 -> x0, waiting for transfers between devices: 3.76 us -> none  [the longest x2 3.75 us: with_halo(): after = lax.ppermute(initial, axis, down)]
    all_to_all x1 -> x0, starting transfers between devices: 3.26 us -> none  [back_to_tiles(): lax.all_to_all(strip_values, 'col', split_axis=1, concat_axis=0, tiled=True)]
    unnamed x25 -> x0, local copies, waits for them, and re-layouts: 3.15 us -> none
  transfers between devices with their start and end apart: 5 -> 0, of which waited for: 2 -> 0; matrix products, arithmetic and copies ran while one was open for 3% -> 0% of each run, Pallas kernels for 0% -> 0%
where the time goes in v1:
time: 24.6 us; the launch traced here: 24.3 us
  blocking collectives  15.4 us (63%)
  Pallas kernels  6.92 us (28%)
  other arithmetic  0.72 us (3%)
  between operations  0.65 us (3%)
  local copies, waits for them, and re-layouts  0.59 us (2%)
    all_to_all x1, blocking collectives, body(): gathered = lax.all_to_all(sent, ('row', 'col'), 0, 0, tiled=True)  15.4 us
    pallas_call x1, Pallas kernels, body(): pl.pallas_call(kernel, out_shape=(jax.ShapeDtypeStruct((own_rows, out_wid...  6.92 us
    convert_element_type x1, other arithmetic, body(): contact_map.astype(jnp.bfloat16).reshape(tile_rows, PATCH, tile_cols, PATCH)  0.72 us

profile of v1, /device:TPU:0, one launch (start us, length us, event | category | flops | bytes accessed | tf_op | source)
XLA Modules:
  0.0 24.3 jit_solution(5457172702574612327)
XLA Ops:
  0.6 0.7 %convert_element_type.3 = bf16[32,64]{1,0:T(8,128)(2,1)S(1)} convert(f32[32,64]{1,0:T(8,128)} %param.13) | non-fusion elementwise | flops 2048 | bytes 12288 | tf_op jit(solution)/shard_map/convert_element_type | solution.py:170
  1.4 0.2 reshape.12
  1.5 0.3 %copy.15 = bf16[4,4,8,16]{3,2,1,0:T(8,128)(2,1)S(1)} copy(bf16[4,4,8,16]{1,3,0,2:T(8,128)(2,1)S(1)} %bitcast.4) | data formatting | bytes 8192 | tf_op jit(solution)/shard_map/transpose | solution.py:171
  1.8 0.1 broadcast_in_dim.7
  2.0 15.4 %all_to_all.5 = bf16[32,16,128]{2,1,0:T(8,128)(2,1)} all-to-all(bf16[32,16,128]{2,1,0:T(8,128)(2,1)S(1)} %broadcast_in_dim.8), channel_id=1, replica_groups=mesh['row'=8,'col'=4] {'row','col'}, dimensions={0} | all-to-all | bytes 262144 | tf_op jit(solution)/shard_map/all_to_all | solution.py:173
  17.4 6.9 %encoder.1 = (bf16[2,256]{1,0:T(2,128)(2,1)}, bf16[8,16,128]{2,1,0:T(8,128)(2,1)}) custom-call(bf16[8,4,16,128]{3,2,1,0:T(8,128)(2,1)} %bitcast.5, bf16[16,128]{1,0:T(8,128)(2,1)} %embed_w.1, f32[128]{0:T(128)} %embed_b.1, bf16[3,3,3,128,128]{4,3,2,1,0:T(8,128)(2,1)} %conv_w.1, f32[3,128]{1,0:T(4,128)} %conv_b.1, bf16[128,128]{1,0:T(8,128)(2,1)} %mix_w.1, ...), custom_call_target="tpu_custom_call" | custom-call | tf_op jit(solution)/shard_map/encoder/pallas_call | solution.py:187
  (1 shorter events, 0.0 us)

commit v2 on v1

--- a/solution.py
+++ b/solution.py
@@ -1,4 +1,5 @@
 import functools
+import itertools
 
 import jax
 import jax.numpy as jnp
@@ -10,7 +11,8 @@
 PATCH = 4
 LAYERS = 3
 UNROLL_CELLS = 2048
-CHUNK_CELLS = 256
+CHUNK_CELLS = 768
+PAD = 8
 
 
 def gelu(x):
@@ -19,19 +21,34 @@
     return half + half * jnp.tanh(x * (scale + (scale * 0.044715) * (x * x)))
 
 
-def for_rows(total, span, step):
+def row_steps(total, span, step):
     if total * span <= UNROLL_CELLS:
         chunk = max(1, CHUNK_CELLS // span)
-        for start in range(0, total, chunk):
-            step(start, min(chunk, total - start))
-    else:
-        lax.fori_loop(0, total, lambda r, carry: (step(r, 1), carry)[1], 0)
+        starts = range(0, total, chunk)
+        return [functools.partial(step, s, min(chunk, total - s)) for s in starts]
+    return [lambda: lax.fori_loop(0, total, lambda r, carry: (step(r, 1), carry)[1], 0)]
+
+
+def in_turn(first, second):
+    for mine, other in itertools.zip_longest(first, second):
+        for thunk in (mine, other):
+            if thunk is not None:
+                thunk()
 
 
 def encoder_kernel(
     gathered, embed_w, embed_b, conv_w, conv_b, mix_w, mix_b, proj_w, proj_b,
     up_w, up_b, down_w, down_b, latents, sym_out, *buffers, tile_rows, tile_cols, shared,
 ):
+    remote = [embed_b, conv_w, mix_b, proj_b, up_b, down_w, down_b]
+    arrived, local, buffers = buffers[0], buffers[1 : 1 + len(remote)], buffers[1 + len(remote) :]
+    loads = [
+        pltpu.make_async_copy(source, target, arrived.at[at])
+        for at, (source, target) in enumerate(zip(remote, local))
+    ]
+    for load in loads:
+        load.start()
+    embed_b, conv_w, mix_b, proj_b, up_b, down_w, down_b = local
     n_row, n_col, pixels, cells = gathered.shape
     width = embed_w.shape[1]
     span = n_row * tile_rows
@@ -44,12 +61,13 @@
         rows = first + lax.broadcasted_iota(jnp.int32, value.shape, 0)
         return jnp.where((rows >= 0) & (rows < span), value, 0.0)
 
-    def emit(target, start, value):
+    def emit(pair, start, value):
+        target, stage = pair
         count = value.shape[0]
-        place = lax.broadcasted_iota(jnp.int32, value.shape, 1)
-        left = jnp.where(place == 0, 0.0, pltpu.roll(value, 1, 1))
-        right = jnp.where(place == span - 1, 0.0, pltpu.roll(value, span - 1, 1))
-        for at, part in enumerate((left, value, right)):
+        base = 0 if shared else start
+        stage[pl.ds(base, count), PAD : PAD + span, :] = value
+        for at in range(3):
+            part = stage[pl.ds(base, count), PAD - 1 + at : PAD - 1 + at + span, :]
             target[pl.ds(start, count), :, at * width : (at + 1) * width] = part.astype(jnp.bfloat16)
 
     def block_weight(group):
@@ -108,7 +126,7 @@
             )
             emit(target, start, keep_inside(value, start + origin))
 
-        for_rows(tile_rows + 2 * LAYERS, span, step)
+        return row_steps(tile_rows + 2 * LAYERS, span, step)
 
     def taps(layer, flipped):
         if flipped:
@@ -116,38 +134,67 @@
         return [conv_w[layer, a].reshape(3 * width, width) for a in range(3)]
 
     def convolve(source, layer, flipped, start, rows, place, extent):
-        total = conv_b[layer : layer + 1, :]
-        for a, weight in enumerate(taps(layer, flipped)):
-            window = source[pl.ds(start + a, rows), pl.ds(place, extent), :]
-            window = window.reshape(rows * extent, 3 * width)
-            total = total + jnp.dot(window, weight, preferred_element_type=jnp.float32)
+        windows = [
+            source[pl.ds(start + a, rows), pl.ds(place, extent), :].reshape(rows * extent, 3 * width)
+            for a in range(3)
+        ]
+        total = jnp.dot(
+            jnp.concatenate(windows, axis=1),
+            jnp.concatenate(taps(layer, flipped), axis=0),
+            preferred_element_type=jnp.float32,
+        )
+        total = total + conv_b[layer : layer + 1, :]
         return gelu(total).reshape(rows, extent, width)
 
-    def features(flipped, first, second, third):
-        embed(first, flipped)
-        for layer, source, target in ((0, first, second), (1, second, third)):
-
-            def step(start, rows, layer=layer, source=source, target=target):
-                value = convolve(source, layer, flipped, start, rows, 0, span)
-                emit(target, start, keep_inside(value, start + origin + layer + 1))
-
-            for_rows(tile_rows + 2 * (LAYERS - layer - 1), span, step)
+    def layer_steps(layer, flipped, source, target):
+        def step(start, rows):
+            value = convolve(source[0], layer, flipped, start, rows, 0, span)
+            emit(target, start, keep_inside(value, start + origin + layer + 1))
+
+        return row_steps(tile_rows + 2 * (LAYERS - layer - 1), span, step)
+
+    def last_layer(flipped, source):
         place = pl.multiple_of(col * tile_cols, tile_cols)
-        tile = convolve(third, LAYERS - 1, flipped, 0, tile_rows, place, tile_cols)
-        strip = convolve(third, LAYERS - 1, flipped, col * own_rows, own_rows, 0, span)
+        tile = convolve(source[0], LAYERS - 1, flipped, 0, tile_rows, place, tile_cols)
+        strip = convolve(source[0], LAYERS - 1, flipped, col * own_rows, own_rows, 0, span)
         return tile.astype(jnp.bfloat16), strip.astype(jnp.bfloat16)
 
     def average(first, second):
         total = first.astype(jnp.float32) + second.astype(jnp.float32)
         return (total * 0.5).astype(jnp.bfloat16)
 
-    one, two, three = buffers[:3]
-    tile, strip = features(False, one, two, three)
+    half = len(buffers) // 2
+    pairs = list(zip(buffers[:half], buffers[half:]))
+    for _, stage in pairs:
+        stage[:, :PAD, :] = jnp.zeros((stage.shape[0], PAD, width), jnp.float32)
+        stage[:, PAD + span :, :] = jnp.zeros((stage.shape[0], PAD, width), jnp.float32)
+    plain, turned = pairs[:LAYERS], pairs[-LAYERS:]
+    loads[0].wait()
     if shared:
-        four, five, six = one, two, three
+        for thunk in embed(plain[0], False):
+            thunk()
+        for load in loads[1:]:
+            load.wait()
+        for layer in range(LAYERS - 1):
+            for thunk in layer_steps(layer, False, plain[layer], plain[layer + 1]):
+                thunk()
+        tile, strip = last_layer(False, plain[-1])
+        for thunk in embed(turned[0], True):
+            thunk()
+        for layer in range(LAYERS - 1):
+            for thunk in layer_steps(layer, True, turned[layer], turned[layer + 1]):
+                thunk()
     else:
-        four, five, six = buffers[3:6]
-    flipped_tile, flipped_strip = features(True, four, five, six)
+        in_turn(embed(plain[0], False), embed(turned[0], True))
+        for load in loads[1:]:
+            load.wait()
+        for layer in range(LAYERS - 1):
+            in_turn(
+                layer_steps(layer, False, plain[layer], plain[layer + 1]),
+                layer_steps(layer, True, turned[layer], turned[layer + 1]),
+            )
+        tile, strip = last_layer(False, plain[-1])
+    flipped_tile, flipped_strip = last_layer(True, turned[-1])
     sym_out[...] = average(tile, flipped_tile)
     sym = average(strip, flipped_strip).reshape(own_rows * span, width)
     mixed = jnp.dot(sym, mix_w[...], preferred_element_type=jnp.float32) + mix_b[...].reshape(1, width)
@@ -178,9 +225,21 @@
     heights = [tile_rows + 2 * (LAYERS - layer) for layer in range(LAYERS)]
     buffers = [pltpu.VMEM((h, span, 3 * width), jnp.bfloat16) for h in heights]
     shared = sum(heights) * span > UNROLL_CELLS * 2
+    stages = [
+        pltpu.VMEM((1 if shared else h, span + 2 * PAD, width), jnp.float32) for h in heights
+    ]
     if not shared:
-        buffers = buffers * 2
+        buffers, stages = buffers * 2, stages * 2
     whole = pl.BlockSpec(memory_space=pltpu.VMEM)
+    operands = [gathered, embed_weight, *rest]
+    in_specs = [whole] * len(operands)
+    copied = []
+    for at in (2, 3, 6, 8, 10, 11, 12):
+        in_specs[at] = pl.BlockSpec(memory_space=pl.ANY)
+        copied.append(pltpu.VMEM(operands[at].shape, operands[at].dtype))
+    for at in range(len(operands)):
+        if in_specs[at] is whole and (at > 0 or not shared):
+            operands[at] = pltpu.with_memory_space_constraint(operands[at], pltpu.VMEM)
     kernel = functools.partial(
         encoder_kernel, tile_rows=tile_rows, tile_cols=tile_cols, shared=shared
     )
@@ -190,11 +249,11 @@
             jax.ShapeDtypeStruct((own_rows, out_width), jnp.bfloat16),
             jax.ShapeDtypeStruct((tile_rows, tile_cols, width), jnp.bfloat16),
         ),
-        in_specs=[whole] * (2 + len(rest)),
+        in_specs=in_specs,
         out_specs=(whole, whole),
-        scratch_shapes=buffers,
+        scratch_shapes=[pltpu.SemaphoreType.DMA((len(copied),))] + copied + buffers + stages,
         name="encoder",
-    )(gathered, embed_weight, *rest)
+    )(*operands)
 
 
 def solution(mesh):

time: 24.6 us -> 23.1 us (0.939)
  Pallas kernels: 6.92 us -> 5.44 us
    pallas_call x1, Pallas kernels: 6.92 us -> 5.44 us  [body(): pl.pallas_call(kernel, out_shape=(jax.ShapeDtypeStruct((own_rows, out_wid...]
where the time goes in v2:
time: 23.1 us; the launch traced here: 22.9 us
  blocking collectives  15.3 us (66%)
  Pallas kernels  5.44 us (24%)
  other arithmetic  0.78 us (3%)
  between operations  0.71 us (3%)
  local copies, waits for them, and re-layouts  0.62 us (3%)
    all_to_all x1, blocking collectives, body(): gathered = lax.all_to_all(sent, ('row', 'col'), 0, 0, tiled=True)  15.3 us
    pallas_call x1, Pallas kernels, body(): pl.pallas_call(kernel, out_shape=(jax.ShapeDtypeStruct((own_rows, out_wid...  5.44 us
    convert_element_type x1, other arithmetic, body(): contact_map.astype(jnp.bfloat16).reshape(tile_rows, PATCH, tile_cols, PATCH)  0.78 us

profile of v2, /device:TPU:0, one launch (start us, length us, event | category | flops | bytes accessed | tf_op | source)
XLA Modules:
  0.0 22.9 jit_solution(18255660084076977192)
XLA Ops:
  0.6 0.0 copy-start
  0.6 0.8 %convert_element_type.3 = bf16[32,64]{1,0:T(8,128)(2,1)S(1)} convert(f32[32,64]{1,0:T(8,128)} %param.13) | non-fusion elementwise | flops 2048 | bytes 12288 | tf_op jit(solution)/shard_map/convert_element_type | solution.py:217
  1.4 0.2 reshape.12
  1.6 0.3 %copy.15 = bf16[4,4,8,16]{3,2,1,0:T(8,128)(2,1)S(1)} copy(bf16[4,4,8,16]{1,3,0,2:T(8,128)(2,1)S(1)} %bitcast.5) | data formatting | bytes 8192 | tf_op jit(solution)/shard_map/transpose | solution.py:218
  1.9 0.1 broadcast_in_dim.7
  2.0 0.0 copy-start.1
  2.0 0.0 copy-start.2
  2.0 0.0 copy-start.3
  2.1 0.0 copy-start.4
  2.1 15.3 %all_to_all.5 = bf16[32,16,128]{2,1,0:T(8,128)(2,1)S(1)} all-to-all(bf16[32,16,128]{2,1,0:T(8,128)(2,1)S(1)} %broadcast_in_dim.8), channel_id=1, replica_groups=mesh['row'=8,'col'=4] {'row','col'}, dimensions={0} | all-to-all | bytes 262144 | tf_op jit(solution)/shard_map/all_to_all | solution.py:220
  17.4 0.0 copy-done
  17.4 0.0 copy-done.1
  17.4 0.0 copy-done.2
  17.4 0.0 copy-done.3
  17.4 0.0 copy-done.4
  17.4 5.4 %encoder.1 = (bf16[2,256]{1,0:T(2,128)(2,1)}, bf16[8,16,128]{2,1,0:T(8,128)(2,1)}) custom-call(bf16[8,4,16,128]{3,2,1,0:T(8,128)(2,1)S(1)} %bitcast.4, bf16[16,128]{1,0:T(8,128)(2,1)S(1)} %copy-done.3, f32[128]{0:T(128)} %embed_b.1, bf16[3,3,3,128,128]{4,3,2,1,0:T(8,128)(2,1)} %conv_w.1, f32[3,128]{1,0:T(4,128)S(1)} %copy-done.4, ...), custom_call_target="tpu_custom_call" | custom-call | tf_op jit(solution)/shard_map/encoder/pallas_call | solution.py:246
  (1 shorter events, 0.0 us)
Async XLA Ops:
  0.6 16.8 %copy-start = (bf16[256,1024]{1,0:T(8,128)(2,1)S(1)}, bf16[256,1024]{1,0:T(8,128)(2,1)}, u32[]{:S(2)}) copy-start(bf16[256,1024]{1,0:T(8,128)(2,1)} %up_w.1) | copy-start | bytes 1572868
  2.0 15.4 %copy-start.1 = (bf16[128,256]{1,0:T(8,128)(2,1)S(1)}, bf16[128,256]{1,0:T(8,128)(2,1)}, u32[]{:S(2)}) copy-start(bf16[128,256]{1,0:T(8,128)(2,1)} %proj_w.1) | copy-start | bytes 196612
  2.0 15.4 %copy-start.2 = (bf16[128,128]{1,0:T(8,128)(2,1)S(1)}, bf16[128,128]{1,0:T(8,128)(2,1)}, u32[]{:S(2)}) copy-start(bf16[128,128]{1,0:T(8,128)(2,1)} %mix_w.1) | copy-start | bytes 98308
  2.0 15.4 %copy-start.3 = (bf16[16,128]{1,0:T(8,128)(2,1)S(1)}, bf16[16,128]{1,0:T(8,128)(2,1)}, u32[]{:S(2)}) copy-start(bf16[16,128]{1,0:T(8,128)(2,1)} %embed_w.1) | copy-start | bytes 12292
  2.1 15.4 %copy-start.4 = (f32[3,128]{1,0:T(4,128)S(1)}, f32[3,128]{1,0:T(4,128)}, u32[]{:S(2)}) copy-start(f32[3,128]{1,0:T(4,128)} %conv_b.1) | copy-start | bytes 4612

commit v3 on v2

v3 whole, which is shorter than its diff:
```python
import functools
import itertools

import jax
import jax.numpy as jnp
from jax import lax
from jax.experimental import pallas as pl
from jax.experimental.pallas import tpu as pltpu
from jax.sharding import PartitionSpec as P

PATCH = 4
LAYERS = 3
UNROLL_CELLS = 2048
CHUNK_CELLS = 768
PAD = 8
PIECE = 32
SLOT = 8


def gelu(x):
    scale = 0.7978845608028654
    half = 0.5 * x
    return half + half * jnp.tanh(x * (scale + (scale * 0.044715) * (x * x)))


def row_steps(total, span, step):
    if total * span <= UNROLL_CELLS:
        chunk = max(1, CHUNK_CELLS // span)
        starts = range(0, total, chunk)
        return [functools.partial(step, s, min(chunk, total - s)) for s in starts]
    return [lambda: lax.fori_loop(0, total, lambda r, carry: (step(r, 1), carry)[1], 0)]


def in_turn(first, second):
    for mine, other in itertools.zip_longest(first, second):
        for thunk in (mine, other):
            if thunk is not None:
                thunk()


def window_tiles(row, flipped, sizes):
    n_row, n_col, tile_rows, tile_cols = sizes
    if not flipped:
        return [row - 1, row, row + 1]
    first = (row * tile_rows - LAYERS + tile_cols) // tile_cols - 1
    starts = [r * tile_rows - LAYERS for r in range(n_row)]
    reach = tile_rows + 2 * LAYERS - 1
    count = max((f + reach) // tile_cols - f // tile_cols + 1 for f in starts)
    return [first + t for t in range(count)]


def selection(row, flipped, start, rows, sizes):
    n_row, n_col, tile_rows, tile_cols = sizes
    inner, outer, limit = (tile_rows, tile_cols, n_col) if flipped else (tile_cols, tile_rows, n_row)
    cells = tile_rows * tile_cols
    shape = (rows, inner, cells)
    major = lax.broadcasted_iota(jnp.int32, shape, 0) + (start + row * tile_rows - LAYERS)
    minor = lax.broadcasted_iota(jnp.int32, shape, 1)
    lane = lax.broadcasted_iota(jnp.int32, shape, 2)
    blocks = []
    for tile in window_tiles(row, flipped, sizes):
        offset = major - tile * outer
        goal = minor * tile_cols + offset if flipped else offset * tile_cols + minor
        ok = (offset >= 0) & (offset < outer) & (major >= 0) & (major < limit * outer)
        block = jnp.where(ok & (lane == goal), 1.0, 0.0)
        blocks.append(block.reshape(rows * inner, cells).astype(jnp.bfloat16))
    return jnp.concatenate(blocks, axis=1)


def split(value, count):
    parts = []
    for _ in range(count):
        part = value.astype(jnp.bfloat16).astype(jnp.float32)
        parts.append(part)
        value = value - part
    return parts


def patch_kernel(tile, sent, *, tile_rows, tile_cols):
    height, span = tile.shape
    cells = tile_rows * tile_cols
    shape = (span, PATCH * cells)
    pixel = lax.broadcasted_iota(jnp.int32, shape, 0)
    lane = lax.broadcasted_iota(jnp.int32, shape, 1)
    goal = (lane % tile_cols) * PATCH + lane // cells
    spread = jnp.where(pixel == goal, 1.0, 0.0).astype(jnp.bfloat16)
    wide = jnp.dot(tile[...].astype(jnp.bfloat16), spread, preferred_element_type=jnp.float32)
    line = lax.broadcasted_iota(jnp.int32, wide.shape, 0) // PATCH
    lane = lax.broadcasted_iota(jnp.int32, wide.shape, 1)
    wide = jnp.where(line == (lane % cells) // tile_cols, wide, 0.0)
    blocks = [wide[:, b * cells : (b + 1) * cells] for b in range(PATCH)]
    stacked = jnp.concatenate(blocks, axis=0).astype(jnp.bfloat16)
    shape = (PATCH * PATCH, PATCH * height)
    pixel = lax.broadcasted_iota(jnp.int32, shape, 0)
    lane = lax.broadcasted_iota(jnp.int32, shape, 1)
    mine = (lane % PATCH == pixel // PATCH) & (lane // height == pixel % PATCH)
    mine = jnp.where(mine, 1.0, 0.0).astype(jnp.bfloat16)
    result = jnp.dot(mine, stacked, preferred_element_type=jnp.float32).astype(jnp.bfloat16)
    sent[...] = jnp.broadcast_to(result[None], sent.shape)


def prepare_kernel(embed_w, embed_b, conv_w, *outs, sizes):
    pixels, width = embed_w.shape
    bias = jnp.concatenate(split(embed_b[...].reshape(1, width), 3), axis=0)
    rest = jnp.zeros((PIECE - pixels - 3, width), jnp.float32)
    left = jnp.concatenate([embed_w[...].astype(jnp.float32), bias, rest], axis=0)
    left = left.astype(jnp.bfloat16)
    products = {}
    for a, b in itertools.product(range(3), range(3)):
        products[a, b] = jnp.dot(left, conv_w[0, a, b], preferred_element_type=jnp.float32)
    for flipped, target in ((False, outs[0]), (True, outs[1])):
        for down in range(3):
            pieces, offsets = [], []
            for along in range(3):
                product = products[(along, down) if flipped else (down, along)]
                pieces += split(product[:pixels], 2)
                offset = jnp.sum(product[pixels : pixels + 3], axis=0, keepdims=True)
                offsets.append(jnp.concatenate(split(offset, 3), axis=0))
                offsets.append(jnp.zeros((SLOT - 3, width), jnp.float32))
            used = 3 * (2 * pixels + SLOT)
            offsets.append(jnp.zeros((width - used, width), jnp.float32))
            value = jnp.concatenate(pieces + offsets, axis=0)
            target[down * width : (down + 1) * width, :] = value.astype(jnp.bfloat16)
    if len(outs) > 2:
        row = lax.axis_index("row")
        for flipped, target in ((False, outs[2]), (True, outs[3])):
            target[...] = selection(row, flipped, 0, sizes[2] + 2 * LAYERS, sizes)


def encoder_kernel(
    gathered, first_plain, first_turned, conv_w, conv_b, mix_w, mix_b, proj_w, proj_b,
    up_w, up_b, down_w, down_b, *refs, sizes, shared,
):
    n_row, n_col, tile_rows, tile_cols = sizes
    if shared:
        selects = (None, None)
    else:
        selects, refs = refs[:2], refs[2:]
    latents, sym_out, refs = refs[0], refs[1], refs[2:]
    remote = [conv_w, mix_b, proj_b, up_b, down_w, down_b]
    arrived, local, buffers = refs[0], refs[1 : 1 + len(remote)], refs[1 + len(remote) :]
    loads = [
        pltpu.make_async_copy(source, target, arrived.at[at])
        for at, (source, target) in enumerate(zip(remote, local))
    ]
    for load in loads:
        load.start()
    conv_w, mix_b, proj_b, up_b, down_w, down_b = local
    _, pixels, cells = gathered.shape
    width = mix_w.shape[0]
    span = n_row * tile_rows
    own_rows = latents.shape[0]
    row = lax.axis_index("row")
    col = lax.axis_index("col")
    origin = row * tile_rows - LAYERS

    def keep_inside(value, first):
        rows = first + lax.broadcasted_iota(jnp.int32, value.shape, 0)
        return jnp.where((rows >= 0) & (rows < span), value, 0.0)

    def shifted(stage, start, value):
        count = value.shape[0]
        base = 0 if shared else start
        stage[pl.ds(base, count), PAD : PAD + span, :] = value
        return [
            stage[pl.ds(base, count), PAD - 1 + at : PAD - 1 + at + span, :] for at in range(3)
        ]

    def emit(pair, start, value):
        target, stage = pair
        for at, part in enumerate(shifted(stage, start, value)):
            lanes = slice(at * width, (at + 1) * width)
            target[pl.ds(start, value.shape[0]), :, lanes] = part.astype(jnp.bfloat16)

    def patches(pair, flipped):
        target, stage = pair
        group, inner = (n_row, tile_rows) if flipped else (n_col, tile_cols)
        limit = (n_col if flipped else n_row) - 1
        ones = jnp.ones((width - 6 * pixels, cells), jnp.bfloat16)
        columns = []
        for tile in window_tiles(row, flipped, sizes):
            at = jnp.clip(tile, 0, limit)
            stacked = []
            for g in range(group):
                source = gathered[g * n_col + at] if flipped else gathered[at * n_col + g]
                stacked += [source] * 6 + [ones]
            columns.append(jnp.concatenate(stacked, axis=0))
        source = jnp.concatenate(columns, axis=1)

        def step(start, rows):
            if shared:
                select = selection(row, flipped, start, rows, sizes)
            else:
                select = selects[flipped][start * inner : (start + rows) * inner, :]
            value = lax.dot_general(
                select, source, (((1,), (1,)), ((), ())), preferred_element_type=jnp.float32
            )
            value = jnp.concatenate(
                [
                    value[:, g * width : (g + 1) * width].reshape(rows, inner, width)
                    for g in range(group)
                ],
                axis=1,
            )
            before, same, after = shifted(stage, start, value)
            lane = lax.broadcasted_iota(jnp.int32, same.shape, 2)
            which = jnp.where(lane < 6 * pixels, lane // (2 * pixels), (lane - 6 * pixels) // SLOT)
            value = jnp.where(which == 0, before, jnp.where(which == 1, same, after))
            target[pl.ds(start, rows), :, :] = value.astype(jnp.bfloat16)

        return row_steps(tile_rows + 2 * LAYERS, span, step)

    def taps(layer, flipped):
        if layer == 0:
            return (first_turned if flipped else first_plain)[...]
        if flipped:
            blocks = [conv_w[layer, :, a].reshape(3 * width, width) for a in range(3)]
            return jnp.concatenate(blocks, axis=0)
        return conv_w[layer].reshape(9 * width, width)

    def convolve(source, layer, flipped, start, rows, place, extent):
        windows = [
            source[pl.ds(start + a, rows), pl.ds(place, extent), :].reshape(rows * extent, -1)
            for a in range(3)
        ]
        total = jnp.dot(
            jnp.concatenate(windows, axis=1),
            taps(layer, flipped),
            preferred_element_type=jnp.float32,
        )
        return gelu(total + conv_b[layer : layer + 1, :]).reshape(rows, extent, width)

    def layer_steps(layer, flipped, source, target):
        def step(start, rows):
            value = convolve(source[0], layer, flipped, start, rows, 0, span)
            emit(target, start, keep_inside(value, start + origin + layer + 1))

        return row_steps(tile_rows + 2 * (LAYERS - layer - 1), span, step)

    def last_strip(flipped, source):
        strip = convolve(source[0], LAYERS - 1, flipped, col * own_rows, own_rows, 0, span)
        return strip.astype(jnp.bfloat16)

    def last_tile(flipped, source):
        place = pl.multiple_of(col * tile_cols, tile_cols)
        tile = convolve(source[0], LAYERS - 1, flipped, 0, tile_rows, place, tile_cols)
        return tile.astype(jnp.bfloat16)

    def average(first, second):
        total = first.astype(jnp.float32) + second.astype(jnp.float32)
        return (total * 0.5).astype(jnp.bfloat16)

    half = len(buffers) // 2
    pairs = list(zip(buffers[:half], buffers[half:]))
    for _, stage in pairs:
        stage[:, :PAD, :] = jnp.zeros((stage.shape[0], PAD, width), jnp.float32)
        stage[:, PAD + span :, :] = jnp.zeros((stage.shape[0], PAD, width), jnp.float32)
    plain, turned = pairs[:LAYERS], pairs[-LAYERS:]
    if shared:
        for load in loads:
            load.wait()
        strips, tiles = [], []
        for flipped, chain in ((False, plain), (True, turned)):
            steps = patches(chain[0], flipped)
            for layer in range(LAYERS - 1):
                steps += layer_steps(layer, flipped, chain[layer], chain[layer + 1])
            for thunk in steps:
                thunk()
            strips.append(last_strip(flipped, chain[-1]))
            tiles.append(last_tile(flipped, chain[-1]))
    else:
        in_turn(patches(plain[0], False), patches(turned[0], True))
        in_turn(
            layer_steps(0, False, plain[0], plain[1]), layer_steps(0, True, turned[0], turned[1])
        )
        for load in loads:
            load.wait()
        for layer in range(1, LAYERS - 1):
            in_turn(
                layer_steps(layer, False, plain[layer], plain[layer + 1]),
                layer_steps(layer, True, turned[layer], turned[layer + 1]),
            )
        strips = [last_strip(False, plain[-1]), last_strip(True, turned[-1])]
        tiles = [last_tile(False, plain[-1]), last_tile(True, turned[-1])]
    sym_out[...] = average(*tiles)
    sym = average(*strips).reshape(own_rows * span, width)
    mixed = jnp.dot(sym, mix_w[...], preferred_element_type=jnp.float32) + mix_b[...].reshape(1, width)
    summed = jnp.sum(gelu(mixed).reshape(own_rows, span, width), axis=1)
    pooled = (summed / span).astype(jnp.bfloat16)
    latent = jnp.dot(pooled, proj_w[...], preferred_element_type=jnp.float32)
    latent = latent + proj_b[...].reshape(1, -1)
    hidden = jnp.dot(latent.astype(jnp.bfloat16), up_w[...], preferred_element_type=jnp.float32)
    hidden = gelu(hidden + up_b[...].reshape(1, -1)).astype(jnp.bfloat16)
    result = jnp.dot(hidden, down_w[...], preferred_element_type=jnp.float32)
    latents[...] = (latent + result + down_b[...].reshape(1, -1)).astype(jnp.bfloat16)


def body(contact_map, embed_weight, embed_bias, conv_weight, *rest):
    n_row, n_col = lax.axis_size("row"), lax.axis_size("col")
    tile_rows = contact_map.shape[0] // PATCH
    tile_cols = contact_map.shape[1] // PATCH
    sizes = (n_row, n_col, tile_rows, tile_cols)
    pixels, width = embed_weight.shape
    cells = tile_rows * tile_cols
    span = n_row * tile_rows
    own_rows = tile_rows // n_col
    out_width = rest[-1].shape[0]
    heights = [tile_rows + 2 * (LAYERS - layer) for layer in range(LAYERS)]
    shared = sum(heights) * span > UNROLL_CELLS * 2
    whole = pl.BlockSpec(memory_space=pltpu.VMEM)

    def near(value):
        return pltpu.with_memory_space_constraint(value, pltpu.VMEM)

    shape = (n_row * n_col, pixels, cells)
    sent = pl.pallas_call(
        functools.partial(patch_kernel, tile_rows=tile_rows, tile_cols=tile_cols),
        out_shape=(jax.ShapeDtypeStruct if shared else pltpu.VMEM)(shape, jnp.bfloat16),
        in_specs=[whole],
        out_specs=whole,
        name="patches",
    )(contact_map)
    gathered = lax.all_to_all(sent, ("row", "col"), 0, 0, tiled=True)
    shapes = [(3 * width, width)] * 2
    if not shared:
        turned_tiles = len(window_tiles(0, True, sizes))
        shapes.append((heights[0] * tile_cols, 3 * cells))
        shapes.append((heights[0] * tile_rows, turned_tiles * cells))
    prepared = pl.pallas_call(
        functools.partial(prepare_kernel, sizes=sizes),
        out_shape=[pltpu.VMEM(shape, jnp.bfloat16) for shape in shapes],
        in_specs=[whole] * 3,
        out_specs=[whole] * len(shapes),
        name="prepare",
    )(embed_weight, embed_bias, conv_weight)
    operands = [gathered, *prepared[:2], conv_weight, *rest, *prepared[2:]]
    in_specs = [whole] * len(operands)
    copied = []
    for at in (3, 6, 8, 10, 11, 12):
        in_specs[at] = pl.BlockSpec(memory_space=pl.ANY)
        copied.append(pltpu.VMEM(operands[at].shape, operands[at].dtype))
    for at in range(len(operands)):
        if in_specs[at] is whole and (2 < at < 13 or at == 0 and not shared):
            operands[at] = near(operands[at])
    buffers = [
        pltpu.VMEM((h, span, width * (3 if at else 1)), jnp.bfloat16) for at, h in enumerate(heights)
    ]
    stages = [
        pltpu.VMEM((1 if shared else h, span + 2 * PAD, width), jnp.float32) for h in heights
    ]
    if not shared:
        buffers, stages = buffers * 2, stages * 2
    return pl.pallas_call(
        functools.partial(encoder_kernel, sizes=sizes, shared=shared),
        out_shape=(
            jax.ShapeDtypeStruct((own_rows, out_width), jnp.bfloat16),
            jax.ShapeDtypeStruct((tile_rows, tile_cols, width), jnp.bfloat16),
        ),
        in_specs=in_specs,
        out_specs=(whole, whole),
        scratch_shapes=[pltpu.SemaphoreType.DMA((len(copied),))] + copied + buffers + stages,
        name="encoder",
    )(*operands)


def solution(mesh):
    return jax.shard_map(
        body,
        mesh=mesh,
        in_specs=(P("row", "col"), P(), P(), P(), P(), P(), P(), P(), P(), P(), P(), P(), P()),
        out_specs=(P(("row", "col"), None), P("row", "col", None)),
        check_vma=False,
    )
```

time: 23.1 us -> 24.1 us (1.043)
  blocking collectives: 15.3 us -> 0 us
  starting transfers between devices: 0 us -> 7.33 us
  waiting for transfers between devices: 0 us -> 4.11 us
  Pallas kernels: 5.44 us -> 8.45 us
  local copies, waits for them, and re-layouts: 0.62 us -> 3.24 us
  other arithmetic: 0.78 us -> 0 us
    all_to_all x1 -> x0, blocking collectives: 15.3 us -> none  [body(): gathered = lax.all_to_all(sent, ('row', 'col'), 0, 0, tiled=True)]
    all_to_all x0 -> x1, starting transfers between devices: none -> 7.33 us  [body(): gathered = lax.all_to_all(sent, ('row', 'col'), 0, 0, tiled=True)]
    all_to_all x0 -> x1, waiting for transfers between devices: none -> 4.11 us  [body(): gathered = lax.all_to_all(sent, ('row', 'col'), 0, 0, tiled=True)]
    unnamed x10 -> x16, local copies, waits for them, and re-layouts: 0.03 us -> 3.24 us
    pallas_call x1 -> x3, Pallas kernels: 5.44 us -> 8.45 us  [the longest x1 5.31 us: body(): pl.pallas_call(functools.partial(encoder_kernel, sizes=sizes, shared=shar...]
    convert_element_type x1 -> x0, other arithmetic: 0.78 us -> none  [body(): contact_map.astype(jnp.bfloat16).reshape(tile_rows, PATCH, tile_cols, PATCH)]
    transpose x1 -> x0, local copies, waits for them, and re-layouts: 0.27 us -> none  [body(): patches = grid.transpose(1, 3, 0, 2).reshape(1, pixels, cells)]
  transfers between devices with their start and end apart: 0 -> 1, of which waited for: 0 -> 1; matrix products, arithmetic and copies ran while one was open for 0% -> 0% of each run, Pallas kernels for 0% -> 6%
where the time goes in v3:
time: 24.1 us; the launch traced here: 23.8 us
  Pallas kernels  8.45 us (35%)
  starting transfers between devices  7.33 us (30%)
  waiting for transfers between devices  4.11 us (17%)
  local copies, waits for them, and re-layouts  3.24 us (13%)
  between operations  0.67 us (3%)
    all_to_all x1, starting transfers between devices, body(): gathered = lax.all_to_all(sent, ('row', 'col'), 0, 0, tiled=True)  7.33 us
    pallas_call x1, Pallas kernels, body(): pl.pallas_call(functools.partial(encoder_kernel, sizes=sizes, shared=shar...  5.31 us
    all_to_all x1, waiting for transfers between devices, body(): gathered = lax.all_to_all(sent, ('row', 'col'), 0, 0, tiled=True)  4.11 us
    unnamed x16, local copies, waits for them, and re-layouts  3.24 us
    pallas_call x1, Pallas kernels, body(): pl.pallas_call(functools.partial(patch_kernel, tile_rows=tile_rows, tile_...  1.63 us
    pallas_call x1, Pallas kernels, body(): pl.pallas_call(functools.partial(prepare_kernel, sizes=sizes), out_shape=...  1.5 us
  transfers between devices with their start and end apart: 1, of which 1 were waited for; matrix products, arithmetic and copies ran while one was open for 0% of the time, Pallas kernels for 6%

profile of v3, /device:TPU:0, one launch (start us, length us, event | category | flops | bytes accessed | tf_op | source)
XLA Modules:
  0.0 23.8 jit_solution(9615100619032633076)
XLA Ops:
  0.6 1.6 %patches.1 = bf16[32,16,128]{2,1,0:T(8,128)(2,1)} custom-call(f32[32,64]{1,0:T(8,128)} %tile.1), custom_call_target="tpu_custom_call" | custom-call | tf_op jit(solution)/shard_map/patches/pallas_call | solution.py:316
  2.3 0.0 copy-start
  2.3 7.3 %all-to-all-start = ((bf16[32,16,128]{2,1,0:T(8,128)(2,1)}), bf16[32,16,128]{2,1,0:T(8,128)(2,1)S(1)}, u32[]{:S(2)}, u32[]{:S(2)}) async-start(bf16[32,16,128]{2,1,0:T(8,128)(2,1)} %patches.1), calls=%async_computation | async-start | bytes 262144 | tf_op jit(solution)/shard_map/all_to_all | solution.py:323
  9.6 0.0 copy-start.4
  9.6 0.0 copy-start.6
  9.6 1.5 %prepare.1 = (bf16[384,128]{1,0:T(8,128)(2,1)S(1)}, bf16[384,128]{1,0:T(8,128)(2,1)S(1)}, bf16[224,384]{1,0:T(8,128)(2,1)S(1)}, bf16[112,256]{1,0:T(8,128)(2,1)S(1)}) custom-call(bf16[16,128]{1,0:T(8,128)(2,1)} %embed_w.1, f32[128]{0:T(128)} %embed_b.1, bf16[3,3,3,128,128]{4,3,2,1,0:T(8,128)(2,1)} %conv_w.3), custom_call_target="tpu_custom_call" | custom-call | tf_op jit(solution)/shard_map/prepare/pallas_call | solution.py:329
  11.1 0.0 copy-start.1
  11.1 0.7 %copy-done.1 = bf16[224,384]{1,0:T(8,128)(2,1)} copy-done((bf16[224,384]{1,0:T(8,128)(2,1)}, bf16[224,384]{1,0:T(8,128)(2,1)S(1)}, u32[]{:S(2)}) %copy-start.1) | copy-done | bytes 172056
  11.8 0.0 copy-start.2
  11.8 0.6 %copy-done.2 = bf16[384,128]{1,0:T(8,128)(2,1)} copy-done((bf16[384,128]{1,0:T(8,128)(2,1)}, bf16[384,128]{1,0:T(8,128)(2,1)S(1)}, u32[]{:S(2)}) %copy-start.2) | copy-done | bytes 98328
  12.4 0.0 copy-start.3
  12.4 0.6 %copy-done.3 = bf16[384,128]{1,0:T(8,128)(2,1)} copy-done((bf16[384,128]{1,0:T(8,128)(2,1)}, bf16[384,128]{1,0:T(8,128)(2,1)S(1)}, u32[]{:S(2)}) %copy-start.3) | copy-done | bytes 98328
  13.1 0.0 copy-start.5
  13.1 0.6 %copy-done.5 = bf16[112,256]{1,0:T(8,128)(2,1)} copy-done((bf16[112,256]{1,0:T(8,128)(2,1)}, bf16[112,256]{1,0:T(8,128)(2,1)S(1)}, u32[]{:S(2)}) %copy-start.5) | copy-done | bytes 57368
  13.7 4.1 %all-to-all-done.gathered = bf16[32,16,128]{2,1,0:T(8,128)(2,1)S(1)} async-done(((bf16[32,16,128]{2,1,0:T(8,128)(2,1)}), bf16[32,16,128]{2,1,0:T(8,128)(2,1)S(1)}, u32[]{:S(2)}, u32[]{:S(2)}) %all-to-all-start) | async-done | bytes 131104 | tf_op jit(solution)/shard_map/all_to_all | solution.py:323
  17.8 0.0 copy-start.7
  17.8 0.0 copy-done
  17.8 0.0 copy-done.4
  17.8 0.0 copy-done.6
  17.8 0.7 %copy-done.7 = f32[3,128]{1,0:T(4,128)S(1)} copy-done((f32[3,128]{1,0:T(4,128)S(1)}, f32[3,128]{1,0:T(4,128)}, u32[]{:S(2)}) %copy-start.7) | copy-done | bytes 1560
  18.5 5.3 %encoder.1 = (bf16[2,256]{1,0:T(2,128)(2,1)}, bf16[8,16,128]{2,1,0:T(8,128)(2,1)}) custom-call(bf16[32,16,128]{2,1,0:T(8,128)(2,1)S(1)} %all-to-all-done.gathered, bf16[384,128]{1,0:T(8,128)(2,1)} %copy-done.2, bf16[384,128]{1,0:T(8,128)(2,1)} %copy-done.3, bf16[3,3,3,128,128]{4,3,2,1,0:T(8,128)(2,1)} %conv_w.3, f32[3,128]{1,0:T(4,128)S(1)} %copy-done.7, ...), custom_call_target="tpu_custom_call" | custom-call | tf_op jit(solution)/shard_map/encoder/pallas_call | solution.py:353
Async XLA Ops:
  2.3 15.5 %copy-start = (bf16[256,1024]{1,0:T(8,128)(2,1)S(1)}, bf16[256,1024]{1,0:T(8,128)(2,1)}, u32[]{:S(2)}) copy-start(bf16[256,1024]{1,0:T(8,128)(2,1)} %up_w.1) | copy-start | bytes 1572868
  2.3 15.5 %all-to-all-start = ((bf16[32,16,128]{2,1,0:T(8,128)(2,1)}), bf16[32,16,128]{2,1,0:T(8,128)(2,1)S(1)}, u32[]{:S(2)}, u32[]{:S(2)}) async-start(bf16[32,16,128]{2,1,0:T(8,128)(2,1)} %patches.1), calls=%async_computation | async-start | bytes 262144 | tf_op jit(solution)/shard_map/all_to_all | solution.py:323
  9.6 8.2 %copy-start.4 = (bf16[128,256]{1,0:T(8,128)(2,1)S(1)}, bf16[128,256]{1,0:T(8,128)(2,1)}, u32[]{:S(2)}) copy-start(bf16[128,256]{1,0:T(8,128)(2,1)} %proj_w.1) | copy-start | bytes 196612
  9.6 8.2 %copy-start.6 = (bf16[128,128]{1,0:T(8,128)(2,1)S(1)}, bf16[128,128]{1,0:T(8,128)(2,1)}, u32[]{:S(2)}) copy-start(bf16[128,128]{1,0:T(8,128)(2,1)} %mix_w.1) | copy-start | bytes 98308
  11.1 0.7 %copy-start.1 = (bf16[224,384]{1,0:T(8,128)(2,1)}, bf16[224,384]{1,0:T(8,128)(2,1)S(1)}, u32[]{:S(2)}) copy-start(bf16[224,384]{1,0:T(8,128)(2,1)S(1)} %get-tuple-element.8.refs_0_) | copy-start | bytes 516100
  11.8 0.6 %copy-start.2 = (bf16[384,128]{1,0:T(8,128)(2,1)}, bf16[384,128]{1,0:T(8,128)(2,1)S(1)}, u32[]{:S(2)}) copy-start(bf16[384,128]{1,0:T(8,128)(2,1)S(1)} %get-tuple-element.6.first_plain) | copy-start | bytes 294916
  12.4 0.6 %copy-start.3 = (bf16[384,128]{1,0:T(8,128)(2,1)}, bf16[384,128]{1,0:T(8,128)(2,1)S(1)}, u32[]{:S(2)}) copy-start(bf16[384,128]{1,0:T(8,128)(2,1)S(1)} %get-tuple-element.7.first_turned) | copy-start | bytes 294916
  13.1 0.6 %copy-start.5 = (bf16[112,256]{1,0:T(8,128)(2,1)}, bf16[112,256]{1,0:T(8,128)(2,1)S(1)}, u32[]{:S(2)}) copy-start(bf16[112,256]{1,0:T(8,128)(2,1)S(1)} %get-tuple-element.9.refs_1_) | copy-start | bytes 172036
  17.8 0.7 %copy-start.7 = (f32[3,128]{1,0:T(4,128)S(1)}, f32[3,128]{1,0:T(4,128)}, u32[]{:S(2)}) copy-start(f32[3,128]{1,0:T(4,128)} %conv_b.1) | copy-start | bytes 4612

commit v4 on v3

--- a/solution.py
+++ b/solution.py
@@ -99,7 +99,26 @@
     sent[...] = jnp.broadcast_to(result[None], sent.shape)
 
 
-def prepare_kernel(embed_w, embed_b, conv_w, *outs, sizes):
+def prepare_kernel(*refs, sizes, count, matrices):
+    embed_w, embed_b, conv_w, *others = refs[:count]
+    outs = refs[count : count + 2 + matrices]
+    kept = refs[count + 2 + matrices : -4]
+    embed_buf, bias_buf, conv_buf, arrived = refs[-4:]
+    sources = [embed_w, embed_b, conv_w.at[0], conv_w.at[pl.ds(1, LAYERS - 1)], *others]
+    targets = [embed_buf, bias_buf, conv_buf, *kept]
+    loads = [
+        pltpu.make_async_copy(source, target, arrived.at[at])
+        for at, (source, target) in enumerate(zip(sources, targets))
+    ]
+    for load in loads:
+        load.start()
+    if matrices:
+        row = lax.axis_index("row")
+        for flipped, target in ((False, outs[2]), (True, outs[3])):
+            target[...] = selection(row, flipped, 0, sizes[2] + 2 * LAYERS, sizes)
+    for load in loads[:3]:
+        load.wait()
+    embed_w, embed_b = embed_buf, bias_buf
     pixels, width = embed_w.shape
     bias = jnp.concatenate(split(embed_b[...].reshape(1, width), 3), axis=0)
     rest = jnp.zeros((PIECE - pixels - 3, width), jnp.float32)
@@ -107,7 +126,7 @@
     left = left.astype(jnp.bfloat16)
     products = {}
     for a, b in itertools.product(range(3), range(3)):
-        products[a, b] = jnp.dot(left, conv_w[0, a, b], preferred_element_type=jnp.float32)
+        products[a, b] = jnp.dot(left, conv_buf[a, b], preferred_element_type=jnp.float32)
     for flipped, target in ((False, outs[0]), (True, outs[1])):
         for down in range(3):
             pieces, offsets = [], []
@@ -121,31 +140,20 @@
             offsets.append(jnp.zeros((width - used, width), jnp.float32))
             value = jnp.concatenate(pieces + offsets, axis=0)
             target[down * width : (down + 1) * width, :] = value.astype(jnp.bfloat16)
-    if len(outs) > 2:
-        row = lax.axis_index("row")
-        for flipped, target in ((False, outs[2]), (True, outs[3])):
-            target[...] = selection(row, flipped, 0, sizes[2] + 2 * LAYERS, sizes)
+    for load in loads[3:]:
+        load.wait()
 
 
 def encoder_kernel(
-    gathered, first_plain, first_turned, conv_w, conv_b, mix_w, mix_b, proj_w, proj_b,
-    up_w, up_b, down_w, down_b, *refs, sizes, shared,
+    gathered, first_plain, first_turned, *refs, sizes, shared,
 ):
     n_row, n_col, tile_rows, tile_cols = sizes
     if shared:
         selects = (None, None)
     else:
         selects, refs = refs[:2], refs[2:]
-    latents, sym_out, refs = refs[0], refs[1], refs[2:]
-    remote = [conv_w, mix_b, proj_b, up_b, down_w, down_b]
-    arrived, local, buffers = refs[0], refs[1 : 1 + len(remote)], refs[1 + len(remote) :]
-    loads = [
-        pltpu.make_async_copy(source, target, arrived.at[at])
-        for at, (source, target) in enumerate(zip(remote, local))
-    ]
-    for load in loads:
-        load.start()
-    conv_w, mix_b, proj_b, up_b, down_w, down_b = local
+    conv_w, conv_b, mix_w, mix_b, proj_w, proj_b, up_w, up_b, down_w, down_b = refs[:10]
+    latents, sym_out, *buffers = refs[10:]
     _, pixels, cells = gathered.shape
     width = mix_w.shape[0]
     span = n_row * tile_rows
@@ -214,9 +222,9 @@
         if layer == 0:
             return (first_turned if flipped else first_plain)[...]
         if flipped:
-            blocks = [conv_w[layer, :, a].reshape(3 * width, width) for a in range(3)]
+            blocks = [conv_w[layer - 1, :, a].reshape(3 * width, width) for a in range(3)]
             return jnp.concatenate(blocks, axis=0)
-        return conv_w[layer].reshape(9 * width, width)
+        return conv_w[layer - 1].reshape(9 * width, width)
 
     def convolve(source, layer, flipped, start, rows, place, extent):
         windows = [
@@ -257,8 +265,6 @@
         stage[:, PAD + span :, :] = jnp.zeros((stage.shape[0], PAD, width), jnp.float32)
     plain, turned = pairs[:LAYERS], pairs[-LAYERS:]
     if shared:
-        for load in loads:
-            load.wait()
         strips, tiles = [], []
         for flipped, chain in ((False, plain), (True, turned)):
             steps = patches(chain[0], flipped)
@@ -273,8 +279,6 @@
         in_turn(
             layer_steps(0, False, plain[0], plain[1]), layer_steps(0, True, turned[0], turned[1])
         )
-        for load in loads:
-            load.wait()
         for layer in range(1, LAYERS - 1):
             in_turn(
                 layer_steps(layer, False, plain[layer], plain[layer + 1]),
@@ -326,22 +330,28 @@
         turned_tiles = len(window_tiles(0, True, sizes))
         shapes.append((heights[0] * tile_cols, 3 * cells))
         shapes.append((heights[0] * tile_rows, turned_tiles * cells))
+    shapes = [pltpu.VMEM(shape, jnp.bfloat16) for shape in shapes]
+    matrices = len(shapes) - 2
+    later = (LAYERS - 1,) + conv_weight.shape[1:]
+    shapes.append(pltpu.VMEM(later, conv_weight.dtype))
+    shapes += [pltpu.VMEM(value.shape, value.dtype) for value in rest]
+    inputs = (embed_weight, embed_bias, conv_weight, *rest)
     prepared = pl.pallas_call(
-        functools.partial(prepare_kernel, sizes=sizes),
-        out_shape=[pltpu.VMEM(shape, jnp.bfloat16) for shape in shapes],
-        in_specs=[whole] * 3,
+        functools.partial(prepare_kernel, sizes=sizes, count=len(inputs), matrices=matrices),
+        out_shape=shapes,
+        in_specs=[pl.BlockSpec(memory_space=pl.ANY)] * len(inputs),
         out_specs=[whole] * len(shapes),
+        scratch_shapes=[
+            pltpu.VMEM(embed_weight.shape, embed_weight.dtype),
+            pltpu.VMEM(embed_bias.shape, embed_bias.dtype),
+            pltpu.VMEM(conv_weight.shape[1:], conv_weight.dtype),
+            pltpu.SemaphoreType.DMA((len(inputs) + 1,)),
+        ],
         name="prepare",
-    )(embed_weight, embed_bias, conv_weight)
-    operands = [gathered, *prepared[:2], conv_weight, *rest, *prepared[2:]]
+    )(*inputs)
+    prepared = [near(value) for value in prepared]
+    operands = [gathered if shared else near(gathered), *prepared]
     in_specs = [whole] * len(operands)
-    copied = []
-    for at in (3, 6, 8, 10, 11, 12):
-        in_specs[at] = pl.BlockSpec(memory_space=pl.ANY)
-        copied.append(pltpu.VMEM(operands[at].shape, operands[at].dtype))
-    for at in range(len(operands)):
-        if in_specs[at] is whole and (2 < at < 13 or at == 0 and not shared):
-            operands[at] = near(operands[at])
     buffers = [
         pltpu.VMEM((h, span, width * (3 if at else 1)), jnp.bfloat16) for at, h in enumerate(heights)
     ]
@@ -358,7 +368,7 @@
         ),
         in_specs=in_specs,
         out_specs=(whole, whole),
-        scratch_shapes=[pltpu.SemaphoreType.DMA((len(copied),))] + copied + buffers + stages,
+        scratch_shapes=buffers + stages,
         name="encoder",
     )(*operands)
 

time: 24.1 us -> 21.8 us (0.905)
  local copies, waits for them, and re-layouts: 3.24 us -> 0 us
  waiting for transfers between devices: 4.11 us -> 6.49 us
  Pallas kernels: 8.45 us -> 6.98 us
    unnamed x16 -> x0, local copies, waits for them, and re-layouts: 3.24 us -> none
    all_to_all x1, waiting for transfers between devices: 4.11 us -> 6.49 us  [body(): gathered = lax.all_to_all(sent, ('row', 'col'), 0, 0, tiled=True)]
    pallas_call x1, Pallas kernels: 5.31 us -> 3.64 us  [body(): pl.pallas_call(functools.partial(encoder_kernel, sizes=sizes, shared=shar...]
  transfers between devices with their start and end apart: 1 -> 1, of which waited for: 1 -> 1; matrix products, arithmetic and copies ran while one was open for 0% -> 0% of each run, Pallas kernels for 6% -> 8%
where the time goes in v4:
time: 21.8 us; the launch traced here: 21.4 us
  starting transfers between devices  7.33 us (34%)
  Pallas kernels  6.98 us (32%)
  waiting for transfers between devices  6.49 us (30%)
  between operations  0.65 us (3%)
    all_to_all x1, starting transfers between devices, body(): gathered = lax.all_to_all(sent, ('row', 'col'), 0, 0, tiled=True)  7.33 us
    all_to_all x1, waiting for transfers between devices, body(): gathered = lax.all_to_all(sent, ('row', 'col'), 0, 0, tiled=True)  6.49 us
    pallas_call x1, Pallas kernels, body(): pl.pallas_call(functools.partial(encoder_kernel, sizes=sizes, shared=shar...  3.64 us
    pallas_call x1, Pallas kernels, body(): pl.pallas_call(functools.partial(prepare_kernel, sizes=sizes, count=len(i...  1.71 us
    pallas_call x1, Pallas kernels, body(): pl.pallas_call(functools.partial(patch_kernel, tile_rows=tile_rows, tile_...  1.64 us
  transfers between devices with their start and end apart: 1, of which 1 were waited for; matrix products, arithmetic and copies ran while one was open for 0% of the time, Pallas kernels for 8%

profile of v4, /device:TPU:0, one launch (start us, length us, event | category | flops | bytes accessed | tf_op | source)
XLA Modules:
  0.0 21.4 jit_solution(13422752775718983032)
XLA Ops:
  0.6 1.6 %patches.1 = bf16[32,16,128]{2,1,0:T(8,128)(2,1)} custom-call(f32[32,64]{1,0:T(8,128)} %tile.1), custom_call_target="tpu_custom_call" | custom-call | tf_op jit(solution)/shard_map/patches/pallas_call | solution.py:320
  2.3 7.3 %all-to-all-start = ((bf16[32,16,128]{2,1,0:T(8,128)(2,1)}), bf16[32,16,128]{2,1,0:T(8,128)(2,1)S(1)}, u32[]{:S(2)}, u32[]{:S(2)}) async-start(bf16[32,16,128]{2,1,0:T(8,128)(2,1)} %patches.1), calls=%async_computation | async-start | bytes 262144 | tf_op jit(solution)/shard_map/all_to_all | solution.py:327
  9.6 1.7 %prepare.1 = (bf16[384,128]{1,0:T(8,128)(2,1)S(1)}, bf16[384,128]{1,0:T(8,128)(2,1)S(1)}, bf16[224,384]{1,0:T(8,128)(2,1)S(1)}, bf16[112,256]{1,0:T(8,128)(2,1)S...) custom-call(bf16[16,128]{1,0:T(8,128)(2,1)} %refs_0_.1, ...), custom_call_target="tpu_custom_call" | custom-call | tf_op jit(solution)/shard_map/prepare/pallas_call | solution.py:339
  11.3 6.5 %all-to-all-done.gathered = bf16[32,16,128]{2,1,0:T(8,128)(2,1)S(1)} async-done(((bf16[32,16,128]{2,1,0:T(8,128)(2,1)}), bf16[32,16,128]{2,1,0:T(8,128)(2,1)S(1)}, u32[]{:S(2)}, u32[]{:S(2)}) %all-to-all-start) | async-done | bytes 131104 | tf_op jit(solution)/shard_map/all_to_all | solution.py:327
  17.8 3.6 %encoder.1 = (bf16[2,256]{1,0:T(2,128)(2,1)}, bf16[8,16,128]{2,1,0:T(8,128)(2,1)}) custom-call(bf16[32,16,128]{2,1,0:T(8,128)(2,1)S(1)} %all-to-all-done.gathered, bf16[384,128]{1,0:T(8,128)(2,1)S(1)} %get-tuple-element.16.first_plain, bf16[384,128]{1,0:T(8,128)(2,1)S(1)} %get-tuple-element.17.first_turned, bf16[224,384]{1,0:T(8,128)(2,1)S(1)} %get-tuple-element.18.refs_0_, ...), custom_call_target="tpu_custom_call" | custom-call | tf_op jit(solution)/shard_map/encoder/pallas_call | solution.py:363
Async XLA Ops:
  2.3 15.5 %all-to-all-start = ((bf16[32,16,128]{2,1,0:T(8,128)(2,1)}), bf16[32,16,128]{2,1,0:T(8,128)(2,1)S(1)}, u32[]{:S(2)}, u32[]{:S(2)}) async-start(bf16[32,16,128]{2,1,0:T(8,128)(2,1)} %patches.1), calls=%async_computation | async-start | bytes 262144 | tf_op jit(solution)/shard_map/all_to_all | solution.py:327

commit v5 on v4

--- a/solution.py
+++ b/solution.py
@@ -15,12 +15,12 @@
 PAD = 8
 PIECE = 32
 SLOT = 8
-
-
-def gelu(x):
-    scale = 0.7978845608028654
-    half = 0.5 * x
-    return half + half * jnp.tanh(x * (scale + (scale * 0.044715) * (x * x)))
+HALVED = (0, 1, 2, 3, 6, 7)
+
+
+def gelu_of_twice(half):
+    scale = 2 * 0.7978845608028654
+    return half + half * jnp.tanh(half * (scale + (4 * scale * 0.044715) * (half * half)))
 
 
 def row_steps(total, span, step):
@@ -123,7 +123,7 @@
     bias = jnp.concatenate(split(embed_b[...].reshape(1, width), 3), axis=0)
     rest = jnp.zeros((PIECE - pixels - 3, width), jnp.float32)
     left = jnp.concatenate([embed_w[...].astype(jnp.float32), bias, rest], axis=0)
-    left = left.astype(jnp.bfloat16)
+    left = (0.5 * left).astype(jnp.bfloat16)
     products = {}
     for a, b in itertools.product(range(3), range(3)):
         products[a, b] = jnp.dot(left, conv_buf[a, b], preferred_element_type=jnp.float32)
@@ -142,6 +142,8 @@
             target[down * width : (down + 1) * width, :] = value.astype(jnp.bfloat16)
     for load in loads[3:]:
         load.wait()
+    for at in HALVED:
+        kept[at][...] = (0.5 * kept[at][...].astype(jnp.float32)).astype(kept[at].dtype)
 
 
 def encoder_kernel(
@@ -160,11 +162,23 @@
     own_rows = latents.shape[0]
     row = lax.axis_index("row")
     col = lax.axis_index("col")
-    origin = row * tile_rows - LAYERS
-
-    def keep_inside(value, first):
-        rows = first + lax.broadcasted_iota(jnp.int32, value.shape, 0)
-        return jnp.where((rows >= 0) & (rows < span), value, 0.0)
+
+    def keep_inside(value, start, margin):
+        rows = value.shape[0]
+        if isinstance(start, int):
+            edges = [max(0, min(rows, edge - start)) for edge in (margin, margin + tile_rows)]
+        else:
+            edges = [rows, rows]
+        pieces = []
+        for low, high in ((0, edges[0]), (edges[1], rows)):
+            first = row * tile_rows - margin + start + low
+            lines = [
+                jnp.where((first + r >= 0) & (first + r < span), value[low + r], 0.0)[None]
+                for r in range(high - low)
+            ]
+            pieces.append(lines)
+        inner = [value[edges[0] : edges[1]]] if edges[1] > edges[0] else []
+        return jnp.concatenate(pieces[0] + inner + pieces[1], axis=0)
 
     def shifted(stage, start, value):
         count = value.shape[0]
@@ -236,23 +250,35 @@
             taps(layer, flipped),
             preferred_element_type=jnp.float32,
         )
-        return gelu(total + conv_b[layer : layer + 1, :]).reshape(rows, extent, width)
+        return gelu_of_twice(total + conv_b[layer : layer + 1, :]).reshape(rows, extent, width)
 
     def layer_steps(layer, flipped, source, target):
         def step(start, rows):
             value = convolve(source[0], layer, flipped, start, rows, 0, span)
-            emit(target, start, keep_inside(value, start + origin + layer + 1))
+            emit(target, start, keep_inside(value, start, LAYERS - layer - 1))
 
         return row_steps(tile_rows + 2 * (LAYERS - layer - 1), span, step)
 
-    def last_strip(flipped, source):
-        strip = convolve(source[0], LAYERS - 1, flipped, col * own_rows, own_rows, 0, span)
-        return strip.astype(jnp.bfloat16)
-
-    def last_tile(flipped, source):
+    def last_layer(flipped, source):
         place = pl.multiple_of(col * tile_cols, tile_cols)
-        tile = convolve(source[0], LAYERS - 1, flipped, 0, tile_rows, place, tile_cols)
-        return tile.astype(jnp.bfloat16)
+        windows = [
+            jnp.concatenate(
+                [
+                    source[0][pl.ds(col * own_rows + a, own_rows), :, :].reshape(own_rows * span, -1),
+                    source[0][a : a + tile_rows, pl.ds(place, tile_cols), :].reshape(cells, -1),
+                ],
+                axis=0,
+            )
+            for a in range(3)
+        ]
+        total = jnp.dot(
+            jnp.concatenate(windows, axis=1),
+            taps(LAYERS - 1, flipped),
+            preferred_element_type=jnp.float32,
+        )
+        total = gelu_of_twice(total + conv_b[LAYERS - 1 :, :]).astype(jnp.bfloat16)
+        strip = total[: own_rows * span].reshape(own_rows, span, width)
+        return strip, total[own_rows * span :].reshape(tile_rows, tile_cols, width)
 
     def average(first, second):
         total = first.astype(jnp.float32) + second.astype(jnp.float32)
@@ -272,8 +298,9 @@
                 steps += layer_steps(layer, flipped, chain[layer], chain[layer + 1])
             for thunk in steps:
                 thunk()
-            strips.append(last_strip(flipped, chain[-1]))
-            tiles.append(last_tile(flipped, chain[-1]))
+            strip, tile = last_layer(flipped, chain[-1])
+            strips.append(strip)
+            tiles.append(tile)
     else:
         in_turn(patches(plain[0], False), patches(turned[0], True))
         in_turn(
@@ -284,17 +311,16 @@
                 layer_steps(layer, False, plain[layer], plain[layer + 1]),
                 layer_steps(layer, True, turned[layer], turned[layer + 1]),
             )
-        strips = [last_strip(False, plain[-1]), last_strip(True, turned[-1])]
-        tiles = [last_tile(False, plain[-1]), last_tile(True, turned[-1])]
+        strips, tiles = zip(last_layer(False, plain[-1]), last_layer(True, turned[-1]))
     sym_out[...] = average(*tiles)
     sym = average(*strips).reshape(own_rows * span, width)
     mixed = jnp.dot(sym, mix_w[...], preferred_element_type=jnp.float32) + mix_b[...].reshape(1, width)
-    summed = jnp.sum(gelu(mixed).reshape(own_rows, span, width), axis=1)
+    summed = jnp.sum(gelu_of_twice(mixed).reshape(own_rows, span, width), axis=1)
     pooled = (summed / span).astype(jnp.bfloat16)
     latent = jnp.dot(pooled, proj_w[...], preferred_element_type=jnp.float32)
     latent = latent + proj_b[...].reshape(1, -1)
     hidden = jnp.dot(latent.astype(jnp.bfloat16), up_w[...], preferred_element_type=jnp.float32)
-    hidden = gelu(hidden + up_b[...].reshape(1, -1)).astype(jnp.bfloat16)
+    hidden = gelu_of_twice(hidden + up_b[...].reshape(1, -1)).astype(jnp.bfloat16)
     result = jnp.dot(hidden, down_w[...], preferred_element_type=jnp.float32)
     latents[...] = (latent + result + down_b[...].reshape(1, -1)).astype(jnp.bfloat16)
 

time: 21.8 us -> 21.8 us (level)
  transfers between devices with their start and end apart: 1 -> 1, of which waited for: 1 -> 1; matrix products, arithmetic and copies ran while one was open for 0% -> 0% of each run, Pallas kernels for 8% -> 9%
where the time goes in v5:
time: 21.8 us; the launch traced here: 21.4 us
  starting transfers between devices  7.33 us (34%)
  Pallas kernels  7.13 us (33%)
  waiting for transfers between devices  6.3 us (29%)
  between operations  0.65 us (3%)
    all_to_all x1, starting transfers between devices, body(): gathered = lax.all_to_all(sent, ('row', 'col'), 0, 0, tiled=True)  7.33 us
    all_to_all x1, waiting for transfers between devices, body(): gathered = lax.all_to_all(sent, ('row', 'col'), 0, 0, tiled=True)  6.3 us
    pallas_call x1, Pallas kernels, body(): pl.pallas_call(functools.partial(encoder_kernel, sizes=sizes, shared=shar...  3.6 us
    pallas_call x1, Pallas kernels, body(): pl.pallas_call(functools.partial(prepare_kernel, sizes=sizes, count=len(i...  1.9 us
    pallas_call x1, Pallas kernels, body(): pl.pallas_call(functools.partial(patch_kernel, tile_rows=tile_rows, tile_...  1.64 us
  transfers between devices with their start and end apart: 1, of which 1 were waited for; matrix products, arithmetic and copies ran while one was open for 0% of the time, Pallas kernels for 9%

profile of v5, /device:TPU:0, one launch (start us, length us, event | category | flops | bytes accessed | tf_op | source)
XLA Modules:
  0.0 21.4 jit_solution(15362989519092685392)
XLA Ops:
  0.6 1.6 %patches.1 = bf16[32,16,128]{2,1,0:T(8,128)(2,1)} custom-call(f32[32,64]{1,0:T(8,128)} %tile.1), custom_call_target="tpu_custom_call" | custom-call | tf_op jit(solution)/shard_map/patches/pallas_call | solution.py:346
  2.3 7.3 %all-to-all-start = ((bf16[32,16,128]{2,1,0:T(8,128)(2,1)}), bf16[32,16,128]{2,1,0:T(8,128)(2,1)S(1)}, u32[]{:S(2)}, u32[]{:S(2)}) async-start(bf16[32,16,128]{2,1,0:T(8,128)(2,1)} %patches.1), calls=%async_computation | async-start | bytes 262144 | tf_op jit(solution)/shard_map/all_to_all | solution.py:353
  9.6 1.9 %prepare.1 = (bf16[384,128]{1,0:T(8,128)(2,1)S(1)}, bf16[384,128]{1,0:T(8,128)(2,1)S(1)}, bf16[224,384]{1,0:T(8,128)(2,1)S(1)}, bf16[112,256]{1,0:T(8,128)(2,1)S...) custom-call(bf16[16,128]{1,0:T(8,128)(2,1)} %refs_0_.1, ...), custom_call_target="tpu_custom_call" | custom-call | tf_op jit(solution)/shard_map/prepare/pallas_call | solution.py:365
  11.5 6.3 %all-to-all-done.gathered = bf16[32,16,128]{2,1,0:T(8,128)(2,1)S(1)} async-done(((bf16[32,16,128]{2,1,0:T(8,128)(2,1)}), bf16[32,16,128]{2,1,0:T(8,128)(2,1)S(1)}, u32[]{:S(2)}, u32[]{:S(2)}) %all-to-all-start) | async-done | bytes 131104 | tf_op jit(solution)/shard_map/all_to_all | solution.py:353
  17.8 3.6 %encoder.1 = (bf16[2,256]{1,0:T(2,128)(2,1)}, bf16[8,16,128]{2,1,0:T(8,128)(2,1)}) custom-call(bf16[32,16,128]{2,1,0:T(8,128)(2,1)S(1)} %all-to-all-done.gathered, bf16[384,128]{1,0:T(8,128)(2,1)S(1)} %get-tuple-element.16.first_plain, bf16[384,128]{1,0:T(8,128)(2,1)S(1)} %get-tuple-element.17.first_turned, bf16[224,384]{1,0:T(8,128)(2,1)S(1)} %get-tuple-element.18.refs_0_, ...), custom_call_target="tpu_custom_call" | custom-call | tf_op jit(solution)/shard_map/encoder/pallas_call | solution.py:389
Async XLA Ops:
  2.3 15.5 %all-to-all-start = ((bf16[32,16,128]{2,1,0:T(8,128)(2,1)}), bf16[32,16,128]{2,1,0:T(8,128)(2,1)S(1)}, u32[]{:S(2)}, u32[]{:S(2)}) async-start(bf16[32,16,128]{2,1,0:T(8,128)(2,1)} %patches.1), calls=%async_computation | async-start | bytes 262144 | tf_op jit(solution)/shard_map/all_to_all | solution.py:353

commit v6 on v5

--- a/solution.py
+++ b/solution.py
@@ -15,7 +15,6 @@
 PAD = 8
 PIECE = 32
 SLOT = 8
-HALVED = (0, 1, 2, 3, 6, 7)
 
 
 def gelu_of_twice(half):
@@ -102,10 +101,12 @@
 def prepare_kernel(*refs, sizes, count, matrices):
     embed_w, embed_b, conv_w, *others = refs[:count]
     outs = refs[count : count + 2 + matrices]
-    kept = refs[count + 2 + matrices : -4]
-    embed_buf, bias_buf, conv_buf, arrived = refs[-4:]
+    kept = refs[count + 2 + matrices : -6]
+    conv_w_kept, conv_b, mix_w, mix_b, proj_w, proj_b, up_w, up_b, _, _ = kept
+    embed_buf, bias_buf, conv_buf, mix_buf, up_buf, arrived = refs[-6:]
     sources = [embed_w, embed_b, conv_w.at[0], conv_w.at[pl.ds(1, LAYERS - 1)], *others]
     targets = [embed_buf, bias_buf, conv_buf, *kept]
+    targets[5], targets[9] = mix_buf, up_buf
     loads = [
         pltpu.make_async_copy(source, target, arrived.at[at])
         for at, (source, target) in enumerate(zip(sources, targets))
@@ -142,8 +143,16 @@
             target[down * width : (down + 1) * width, :] = value.astype(jnp.bfloat16)
     for load in loads[3:]:
         load.wait()
-    for at in HALVED:
-        kept[at][...] = (0.5 * kept[at][...].astype(jnp.float32)).astype(kept[at].dtype)
+    for ref in (conv_w_kept, conv_b, mix_b):
+        ref[...] = (0.5 * ref[...].astype(jnp.float32)).astype(ref.dtype)
+    quarter = (0.25 * mix_buf[...].astype(jnp.float32)).astype(jnp.bfloat16)
+    mix_w[...] = jnp.concatenate([quarter, quarter], axis=0)
+    half = (0.5 * up_buf[...].astype(jnp.float32)).astype(jnp.bfloat16)
+    joint = jnp.dot(proj_w[...], half, preferred_element_type=jnp.float32)
+    up_w[...] = jnp.concatenate(split(joint, 2), axis=0).astype(jnp.bfloat16)
+    pieces = jnp.concatenate(split(proj_b[...].reshape(1, -1), 3), axis=0).astype(jnp.bfloat16)
+    shift = jnp.dot(pieces, half, preferred_element_type=jnp.float32)
+    up_b[...] = 0.5 * up_b[...] + jnp.sum(shift, axis=0)
 
 
 def encoder_kernel(
@@ -157,7 +166,7 @@
     conv_w, conv_b, mix_w, mix_b, proj_w, proj_b, up_w, up_b, down_w, down_b = refs[:10]
     latents, sym_out, *buffers = refs[10:]
     _, pixels, cells = gathered.shape
-    width = mix_w.shape[0]
+    width = mix_w.shape[1]
     span = n_row * tile_rows
     own_rows = latents.shape[0]
     row = lax.axis_index("row")
@@ -204,7 +213,7 @@
             at = jnp.clip(tile, 0, limit)
             stacked = []
             for g in range(group):
-                source = gathered[g * n_col + at] if flipped else gathered[at * n_col + g]
+                source = gathered[at * n_row + g] if flipped else gathered[g * n_row + at]
                 stacked += [source] * 6 + [ones]
             columns.append(jnp.concatenate(stacked, axis=0))
         source = jnp.concatenate(columns, axis=1)
@@ -313,13 +322,14 @@
             )
         strips, tiles = zip(last_layer(False, plain[-1]), last_layer(True, turned[-1]))
     sym_out[...] = average(*tiles)
-    sym = average(*strips).reshape(own_rows * span, width)
-    mixed = jnp.dot(sym, mix_w[...], preferred_element_type=jnp.float32) + mix_b[...].reshape(1, width)
+    both = jnp.concatenate([s.reshape(own_rows * span, width) for s in strips], axis=1)
+    mixed = jnp.dot(both, mix_w[...], preferred_element_type=jnp.float32) + mix_b[...].reshape(1, width)
     summed = jnp.sum(gelu_of_twice(mixed).reshape(own_rows, span, width), axis=1)
     pooled = (summed / span).astype(jnp.bfloat16)
     latent = jnp.dot(pooled, proj_w[...], preferred_element_type=jnp.float32)
     latent = latent + proj_b[...].reshape(1, -1)
-    hidden = jnp.dot(latent.astype(jnp.bfloat16), up_w[...], preferred_element_type=jnp.float32)
+    twice = jnp.concatenate([pooled, pooled], axis=1)
+    hidden = jnp.dot(twice, up_w[...], preferred_element_type=jnp.float32)
     hidden = gelu_of_twice(hidden + up_b[...].reshape(1, -1)).astype(jnp.bfloat16)
     result = jnp.dot(hidden, down_w[...], preferred_element_type=jnp.float32)
     latents[...] = (latent + result + down_b[...].reshape(1, -1)).astype(jnp.bfloat16)
@@ -350,7 +360,7 @@
         out_specs=whole,
         name="patches",
     )(contact_map)
-    gathered = lax.all_to_all(sent, ("row", "col"), 0, 0, tiled=True)
+    gathered = lax.all_to_all(sent, ("col", "row"), 0, 0, tiled=True)
     shapes = [(3 * width, width)] * 2
     if not shared:
         turned_tiles = len(window_tiles(0, True, sizes))
@@ -361,6 +371,9 @@
     later = (LAYERS - 1,) + conv_weight.shape[1:]
     shapes.append(pltpu.VMEM(later, conv_weight.dtype))
     shapes += [pltpu.VMEM(value.shape, value.dtype) for value in rest]
+    mix_weight, up_weight = rest[1], rest[5]
+    shapes[matrices + 4] = pltpu.VMEM((2 * width, width), jnp.bfloat16)
+    shapes[matrices + 8] = pltpu.VMEM((2 * width, up_weight.shape[1]), jnp.bfloat16)
     inputs = (embed_weight, embed_bias, conv_weight, *rest)
     prepared = pl.pallas_call(
         functools.partial(prepare_kernel, sizes=sizes, count=len(inputs), matrices=matrices),
@@ -371,6 +384,8 @@
             pltpu.VMEM(embed_weight.shape, embed_weight.dtype),
             pltpu.VMEM(embed_bias.shape, embed_bias.dtype),
             pltpu.VMEM(conv_weight.shape[1:], conv_weight.dtype),
+            pltpu.VMEM(mix_weight.shape, mix_weight.dtype),
+            pltpu.VMEM(up_weight.shape, up_weight.dtype),
             pltpu.SemaphoreType.DMA((len(inputs) + 1,)),
         ],
         name="prepare",

time: 21.8 us -> 21.3 us (0.977)
  waiting for transfers between devices: 6.3 us -> 5.57 us
  Pallas kernels: 7.13 us -> 7.38 us
    all_to_all x1, waiting for transfers between devices: 6.3 us -> 5.57 us  [body(): gathered = lax.all_to_all(sent, ('col', 'row'), 0, 0, tiled=True)]
    pallas_call x1, Pallas kernels: 1.9 us -> 2.23 us  [body(): pl.pallas_call(functools.partial(prepare_kernel, sizes=sizes, count=len(i...]
  transfers between devices with their start and end apart: 1 -> 1, of which waited for: 1 -> 1; matrix products, arithmetic and copies ran while one was open for 0% -> 0% of each run, Pallas kernels for 9% -> 11%
where the time goes in v6:
time: 21.3 us; the launch traced here: 20.9 us
  Pallas kernels  7.38 us (35%)
  starting transfers between devices  7.33 us (34%)
  waiting for transfers between devices  5.57 us (26%)
  between operations  0.65 us (3%)
    all_to_all x1, starting transfers between devices, body(): gathered = lax.all_to_all(sent, ('col', 'row'), 0, 0, tiled=True)  7.33 us
    all_to_all x1, waiting for transfers between devices, body(): gathered = lax.all_to_all(sent, ('col', 'row'), 0, 0, tiled=True)  5.57 us
    pallas_call x1, Pallas kernels, body(): pl.pallas_call(functools.partial(encoder_kernel, sizes=sizes, shared=shar...  3.52 us
    pallas_call x1, Pallas kernels, body(): pl.pallas_call(functools.partial(prepare_kernel, sizes=sizes, count=len(i...  2.23 us
    pallas_call x1, Pallas kernels, body(): pl.pallas_call(functools.partial(patch_kernel, tile_rows=tile_rows, tile_...  1.64 us
  transfers between devices with their start and end apart: 1, of which 1 were waited for; matrix products, arithmetic and copies ran while one was open for 0% of the time, Pallas kernels for 11%

profile of v6, /device:TPU:0, one launch (start us, length us, event | category | flops | bytes accessed | tf_op | source)
XLA Modules:
  0.0 20.9 jit_solution(273170635520452370)
XLA Ops:
  0.6 1.6 %patches.1 = bf16[32,16,128]{2,1,0:T(8,128)(2,1)} custom-call(f32[32,64]{1,0:T(8,128)} %tile.1), custom_call_target="tpu_custom_call" | custom-call | tf_op jit(solution)/shard_map/patches/pallas_call | solution.py:356
  2.3 7.3 %all-to-all-start = ((bf16[32,16,128]{2,1,0:T(8,128)(2,1)}), bf16[32,16,128]{2,1,0:T(8,128)(2,1)S(1)}, u32[]{:S(2)}, u32[]{:S(2)}) async-start(bf16[32,16,128]{2,1,0:T(8,128)(2,1)} %patches.1), calls=%async_computation | async-start | bytes 262144 | tf_op jit(solution)/shard_map/all_to_all | solution.py:363
  9.6 2.2 %prepare.1 = (bf16[384,128]{1,0:T(8,128)(2,1)S(1)}, bf16[384,128]{1,0:T(8,128)(2,1)S(1)}, bf16[224,384]{1,0:T(8,128)(2,1)S(1)}, bf16[112,256]{1,0:T(8,128)(2,1)S...) custom-call(bf16[16,128]{1,0:T(8,128)(2,1)} %refs_0_.1, ...), custom_call_target="tpu_custom_call" | custom-call | tf_op jit(solution)/shard_map/prepare/pallas_call | solution.py:378
  11.8 5.6 %all-to-all-done.gathered = bf16[32,16,128]{2,1,0:T(8,128)(2,1)S(1)} async-done(((bf16[32,16,128]{2,1,0:T(8,128)(2,1)}), bf16[32,16,128]{2,1,0:T(8,128)(2,1)S(1)}, u32[]{:S(2)}, u32[]{:S(2)}) %all-to-all-start) | async-done | bytes 131104 | tf_op jit(solution)/shard_map/all_to_all | solution.py:363
  17.4 3.5 %encoder.1 = (bf16[2,256]{1,0:T(2,128)(2,1)}, bf16[8,16,128]{2,1,0:T(8,128)(2,1)}) custom-call(bf16[32,16,128]{2,1,0:T(8,128)(2,1)S(1)} %all-to-all-done.gathered, bf16[384,128]{1,0:T(8,128)(2,1)S(1)} %get-tuple-element.16.first_plain, bf16[384,128]{1,0:T(8,128)(2,1)S(1)} %get-tuple-element.17.first_turned, bf16[224,384]{1,0:T(8,128)(2,1)S(1)} %get-tuple-element.18.refs_0_, ...), custom_call_target="tpu_custom_call" | custom-call | tf_op jit(solution)/shard_map/encoder/pallas_call | solution.py:404
Async XLA Ops:
  2.3 15.1 %all-to-all-start = ((bf16[32,16,128]{2,1,0:T(8,128)(2,1)}), bf16[32,16,128]{2,1,0:T(8,128)(2,1)S(1)}, u32[]{:S(2)}, u32[]{:S(2)}) async-start(bf16[32,16,128]{2,1,0:T(8,128)(2,1)} %patches.1), calls=%async_computation | async-start | bytes 262144 | tf_op jit(solution)/shard_map/all_to_all | solution.py:363

commit v7 on v6

--- a/solution.py
+++ b/solution.py
@@ -11,7 +11,7 @@
 PATCH = 4
 LAYERS = 3
 UNROLL_CELLS = 2048
-CHUNK_CELLS = 768
+CHUNK_CELLS = 1024
 PAD = 8
 PIECE = 32
 SLOT = 8
@@ -117,9 +117,10 @@
         row = lax.axis_index("row")
         for flipped, target in ((False, outs[2]), (True, outs[3])):
             target[...] = selection(row, flipped, 0, sizes[2] + 2 * LAYERS, sizes)
-    for load in loads[:3]:
+    for load in loads[:3] + loads[4:5]:
         load.wait()
     embed_w, embed_b = embed_buf, bias_buf
+    first_bias = conv_b[0:1, :]
     pixels, width = embed_w.shape
     bias = jnp.concatenate(split(embed_b[...].reshape(1, width), 3), axis=0)
     rest = jnp.zeros((PIECE - pixels - 3, width), jnp.float32)
@@ -135,13 +136,15 @@
                 product = products[(along, down) if flipped else (down, along)]
                 pieces += split(product[:pixels], 2)
                 offset = jnp.sum(product[pixels : pixels + 3], axis=0, keepdims=True)
+                if (down, along) == (1, 1):
+                    offset = offset + 0.5 * first_bias
                 offsets.append(jnp.concatenate(split(offset, 3), axis=0))
                 offsets.append(jnp.zeros((SLOT - 3, width), jnp.float32))
             used = 3 * (2 * pixels + SLOT)
             offsets.append(jnp.zeros((width - used, width), jnp.float32))
             value = jnp.concatenate(pieces + offsets, axis=0)
             target[down * width : (down + 1) * width, :] = value.astype(jnp.bfloat16)
-    for load in loads[3:]:
+    for load in loads[3:4] + loads[5:]:
         load.wait()
     for ref in (conv_w_kept, conv_b, mix_b):
         ref[...] = (0.5 * ref[...].astype(jnp.float32)).astype(ref.dtype)
@@ -259,7 +262,9 @@
             taps(layer, flipped),
             preferred_element_type=jnp.float32,
         )
-        return gelu_of_twice(total + conv_b[layer : layer + 1, :]).reshape(rows, extent, width)
+        if layer > 0:
+            total = total + conv_b[layer : layer + 1, :]
+        return gelu_of_twice(total).reshape(rows, extent, width)
 
     def layer_steps(layer, flipped, source, target):
         def step(start, rows):

time: 21.3 us -> 21 us (0.986)
  Pallas kernels: 7.38 us -> 7.12 us
    pallas_call x1, Pallas kernels: 3.52 us -> 3.26 us  [body(): pl.pallas_call(functools.partial(encoder_kernel, sizes=sizes, shared=shar...]
where the time goes in v7:
time: 21 us; the launch traced here: 20.7 us
  starting transfers between devices  7.33 us (35%)
  Pallas kernels  7.12 us (34%)
  waiting for transfers between devices  5.57 us (27%)
  between operations  0.65 us (3%)
    all_to_all x1, starting transfers between devices, body(): gathered = lax.all_to_all(sent, ('col', 'row'), 0, 0, tiled=True)  7.33 us
    all_to_all x1, waiting for transfers between devices, body(): gathered = lax.all_to_all(sent, ('col', 'row'), 0, 0, tiled=True)  5.57 us
    pallas_call x1, Pallas kernels, body(): pl.pallas_call(functools.partial(encoder_kernel, sizes=sizes, shared=shar...  3.26 us
    pallas_call x1, Pallas kernels, body(): pl.pallas_call(functools.partial(prepare_kernel, sizes=sizes, count=len(i...  2.23 us
    pallas_call x1, Pallas kernels, body(): pl.pallas_call(functools.partial(patch_kernel, tile_rows=tile_rows, tile_...  1.64 us
  transfers between devices with their start and end apart: 1, of which 1 were waited for; matrix products, arithmetic and copies ran while one was open for 0% of the time, Pallas kernels for 11%

profile of v7, /device:TPU:0, one launch (start us, length us, event | category | flops | bytes accessed | tf_op | source)
XLA Modules:
  0.0 20.7 jit_solution(6812070791619106723)
XLA Ops:
  0.6 1.6 %patches.1 = bf16[32,16,128]{2,1,0:T(8,128)(2,1)} custom-call(f32[32,64]{1,0:T(8,128)} %tile.1), custom_call_target="tpu_custom_call" | custom-call | tf_op jit(solution)/shard_map/patches/pallas_call | solution.py:361
  2.3 7.3 %all-to-all-start = ((bf16[32,16,128]{2,1,0:T(8,128)(2,1)}), bf16[32,16,128]{2,1,0:T(8,128)(2,1)S(1)}, u32[]{:S(2)}, u32[]{:S(2)}) async-start(bf16[32,16,128]{2,1,0:T(8,128)(2,1)} %patches.1), calls=%async_computation | async-start | bytes 262144 | tf_op jit(solution)/shard_map/all_to_all | solution.py:368
  9.6 2.2 %prepare.1 = (bf16[384,128]{1,0:T(8,128)(2,1)S(1)}, bf16[384,128]{1,0:T(8,128)(2,1)S(1)}, bf16[224,384]{1,0:T(8,128)(2,1)S(1)}, bf16[112,256]{1,0:T(8,128)(2,1)S...) custom-call(bf16[16,128]{1,0:T(8,128)(2,1)} %refs_0_.1, ...), custom_call_target="tpu_custom_call" | custom-call | tf_op jit(solution)/shard_map/prepare/pallas_call | solution.py:383
  11.8 5.6 %all-to-all-done.gathered = bf16[32,16,128]{2,1,0:T(8,128)(2,1)S(1)} async-done(((bf16[32,16,128]{2,1,0:T(8,128)(2,1)}), bf16[32,16,128]{2,1,0:T(8,128)(2,1)S(1)}, u32[]{:S(2)}, u32[]{:S(2)}) %all-to-all-start) | async-done | bytes 131104 | tf_op jit(solution)/shard_map/all_to_all | solution.py:368
  17.4 3.3 %encoder.1 = (bf16[2,256]{1,0:T(2,128)(2,1)}, bf16[8,16,128]{2,1,0:T(8,128)(2,1)}) custom-call(bf16[32,16,128]{2,1,0:T(8,128)(2,1)S(1)} %all-to-all-done.gathered, bf16[384,128]{1,0:T(8,128)(2,1)S(1)} %get-tuple-element.16.first_plain, bf16[384,128]{1,0:T(8,128)(2,1)S(1)} %get-tuple-element.17.first_turned, bf16[224,384]{1,0:T(8,128)(2,1)S(1)} %get-tuple-element.18.refs_0_, ...), custom_call_target="tpu_custom_call" | custom-call | tf_op jit(solution)/shard_map/encoder/pallas_call | solution.py:409
Async XLA Ops:
  2.3 15.1 %all-to-all-start = ((bf16[32,16,128]{2,1,0:T(8,128)(2,1)}), bf16[32,16,128]{2,1,0:T(8,128)(2,1)S(1)}, u32[]{:S(2)}, u32[]{:S(2)}) async-start(bf16[32,16,128]{2,1,0:T(8,128)(2,1)} %patches.1), calls=%async_computation | async-start | bytes 262144 | tf_op jit(solution)/shard_map/all_to_all | solution.py:368

commit v8 on v7

--- a/solution.py
+++ b/solution.py
@@ -62,8 +62,10 @@
         goal = minor * tile_cols + offset if flipped else offset * tile_cols + minor
         ok = (offset >= 0) & (offset < outer) & (major >= 0) & (major < limit * outer)
         block = jnp.where(ok & (lane == goal), 1.0, 0.0)
-        blocks.append(block.reshape(rows * inner, cells).astype(jnp.bfloat16))
-    return jnp.concatenate(blocks, axis=1)
+        blocks.append(block.reshape(rows * inner, cells))
+    if not flipped:
+        blocks = [blocks[1], blocks[0] + blocks[2]]
+    return jnp.concatenate([block.astype(jnp.bfloat16) for block in blocks], axis=1)
 
 
 def split(value, count):
@@ -211,14 +213,23 @@
         group, inner = (n_row, tile_rows) if flipped else (n_col, tile_cols)
         limit = (n_col if flipped else n_row) - 1
         ones = jnp.ones((width - 6 * pixels, cells), jnp.bfloat16)
-        columns = []
-        for tile in window_tiles(row, flipped, sizes):
+        columns = [[] for _ in window_tiles(row, flipped, sizes)]
+        for column, tile in zip(columns, window_tiles(row, flipped, sizes)):
             at = jnp.clip(tile, 0, limit)
-            stacked = []
             for g in range(group):
-                source = gathered[at * n_row + g] if flipped else gathered[g * n_row + at]
-                stacked += [source] * 6 + [ones]
-            columns.append(jnp.concatenate(stacked, axis=0))
+                column.append(gathered[at * n_row + g] if flipped else gathered[g * n_row + at])
+        if not flipped:
+            lane = lax.broadcasted_iota(jnp.int32, (pixels, cells), 1)
+            late = lane >= (tile_rows - LAYERS) * tile_cols
+            rims = [
+                jnp.where(late, up.astype(jnp.float32), down.astype(jnp.float32))
+                for up, down in zip(columns[0], columns[2])
+            ]
+            columns = [columns[1], [rim.astype(jnp.bfloat16) for rim in rims]]
+        columns = [
+            jnp.concatenate([part for tile in column for part in [tile] * 6 + [ones]], axis=0)
+            for column in columns
+        ]
         source = jnp.concatenate(columns, axis=1)
 
         def step(start, rows):
@@ -273,26 +284,14 @@
 
         return row_steps(tile_rows + 2 * (LAYERS - layer - 1), span, step)
 
-    def last_layer(flipped, source):
+    def last_strip(flipped, source):
+        strip = convolve(source[0], LAYERS - 1, flipped, col * own_rows, own_rows, 0, span)
+        return strip.astype(jnp.bfloat16)
+
+    def last_tile(flipped, source):
         place = pl.multiple_of(col * tile_cols, tile_cols)
-        windows = [
-            jnp.concatenate(
-                [
-                    source[0][pl.ds(col * own_rows + a, own_rows), :, :].reshape(own_rows * span, -1),
-                    source[0][a : a + tile_rows, pl.ds(place, tile_cols), :].reshape(cells, -1),
-                ],
-                axis=0,
-            )
-            for a in range(3)
-        ]
-        total = jnp.dot(
-            jnp.concatenate(windows, axis=1),
-            taps(LAYERS - 1, flipped),
-            preferred_element_type=jnp.float32,
-        )
-        total = gelu_of_twice(total + conv_b[LAYERS - 1 :, :]).astype(jnp.bfloat16)
-        strip = total[: own_rows * span].reshape(own_rows, span, width)
-        return strip, total[own_rows * span :].reshape(tile_rows, tile_cols, width)
+        tile = convolve(source[0], LAYERS - 1, flipped, 0, tile_rows, place, tile_cols)
+        return tile.astype(jnp.bfloat16)
 
     def average(first, second):
         total = first.astype(jnp.float32) + second.astype(jnp.float32)
@@ -312,20 +311,19 @@
                 steps += layer_steps(layer, flipped, chain[layer], chain[layer + 1])
             for thunk in steps:
                 thunk()
-            strip, tile = last_layer(flipped, chain[-1])
-            strips.append(strip)
-            tiles.append(tile)
+            strips.append(last_strip(flipped, chain[-1]))
+            tiles.append(last_tile(flipped, chain[-1]))
     else:
         in_turn(patches(plain[0], False), patches(turned[0], True))
-        in_turn(
-            layer_steps(0, False, plain[0], plain[1]), layer_steps(0, True, turned[0], turned[1])
-        )
-        for layer in range(1, LAYERS - 1):
-            in_turn(
-                layer_steps(layer, False, plain[layer], plain[layer + 1]),
-                layer_steps(layer, True, turned[layer], turned[layer + 1]),
-            )
-        strips, tiles = zip(last_layer(False, plain[-1]), last_layer(True, turned[-1]))
+        in_turn(layer_steps(0, False, plain[0], plain[1]), [])
+        in_turn(layer_steps(0, True, turned[0], turned[1]), [])
+        in_turn(layer_steps(1, False, plain[1], plain[2]), [])
+        in_turn(layer_steps(1, True, turned[1], turned[2]), [])
+        strip_m = last_strip(False, plain[-1])
+        tile_m = last_tile(False, plain[-1])
+        strip_t = last_strip(True, turned[-1])
+        tile_t = last_tile(True, turned[-1])
+        strips, tiles = [strip_m, strip_t], [tile_m, tile_t]
     sym_out[...] = average(*tiles)
     both = jnp.concatenate([s.reshape(own_rows * span, width) for s in strips], axis=1)
     mixed = jnp.dot(both, mix_w[...], preferred_element_type=jnp.float32) + mix_b[...].reshape(1, width)
@@ -369,7 +367,7 @@
     shapes = [(3 * width, width)] * 2
     if not shared:
         turned_tiles = len(window_tiles(0, True, sizes))
-        shapes.append((heights[0] * tile_cols, 3 * cells))
+        shapes.append((heights[0] * tile_cols, 2 * cells))
         shapes.append((heights[0] * tile_rows, turned_tiles * cells))
     shapes = [pltpu.VMEM(shape, jnp.bfloat16) for shape in shapes]
     matrices = len(shapes) - 2

time: 21 us -> 21 us (level)
  no operation moved by 1% of the time
where the time goes in v8:
time: 21 us; the launch traced here: 20.6 us
  starting transfers between devices  7.33 us (35%)
  Pallas kernels  7.04 us (34%)
  waiting for transfers between devices  5.57 us (27%)
  between operations  0.65 us (3%)
    all_to_all x1, starting transfers between devices, body(): gathered = lax.all_to_all(sent, ('col', 'row'), 0, 0, tiled=True)  7.33 us
    all_to_all x1, waiting for transfers between devices, body(): gathered = lax.all_to_all(sent, ('col', 'row'), 0, 0, tiled=True)  5.57 us
    pallas_call x1, Pallas kernels, body(): pl.pallas_call(functools.partial(encoder_kernel, sizes=sizes, shared=shar...  3.18 us
    pallas_call x1, Pallas kernels, body(): pl.pallas_call(functools.partial(prepare_kernel, sizes=sizes, count=len(i...  2.23 us
    pallas_call x1, Pallas kernels, body(): pl.pallas_call(functools.partial(patch_kernel, tile_rows=tile_rows, tile_...  1.64 us
  transfers between devices with their start and end apart: 1, of which 1 were waited for; matrix products, arithmetic and copies ran while one was open for 0% of the time, Pallas kernels for 11%

profile of v8, /device:TPU:0, one launch (start us, length us, event | category | flops | bytes accessed | tf_op | source)
XLA Modules:
  0.0 20.6 jit_solution(7776810907969245303)
XLA Ops:
  0.6 1.6 %patches.1 = bf16[32,16,128]{2,1,0:T(8,128)(2,1)} custom-call(f32[32,64]{1,0:T(8,128)} %tile.1), custom_call_target="tpu_custom_call" | custom-call | tf_op jit(solution)/shard_map/patches/pallas_call | solution.py:359
  2.3 7.3 %all-to-all-start = ((bf16[32,16,128]{2,1,0:T(8,128)(2,1)}), bf16[32,16,128]{2,1,0:T(8,128)(2,1)S(1)}, u32[]{:S(2)}, u32[]{:S(2)}) async-start(bf16[32,16,128]{2,1,0:T(8,128)(2,1)} %patches.1), calls=%async_computation | async-start | bytes 262144 | tf_op jit(solution)/shard_map/all_to_all | solution.py:366
  9.6 2.2 %prepare.1 = (bf16[384,128]{1,0:T(8,128)(2,1)S(1)}, bf16[384,128]{1,0:T(8,128)(2,1)S(1)}, bf16[224,256]{1,0:T(8,128)(2,1)S(1)}, bf16[112,256]{1,0:T(8,128)(2,1)S...) custom-call(bf16[16,128]{1,0:T(8,128)(2,1)} %refs_0_.1, ...), custom_call_target="tpu_custom_call" | custom-call | tf_op jit(solution)/shard_map/prepare/pallas_call | solution.py:381
  11.8 5.6 %all-to-all-done.gathered = bf16[32,16,128]{2,1,0:T(8,128)(2,1)S(1)} async-done(((bf16[32,16,128]{2,1,0:T(8,128)(2,1)}), bf16[32,16,128]{2,1,0:T(8,128)(2,1)S(1)}, u32[]{:S(2)}, u32[]{:S(2)}) %all-to-all-start) | async-done | bytes 131104 | tf_op jit(solution)/shard_map/all_to_all | solution.py:366
  17.4 3.2 %encoder.1 = (bf16[2,256]{1,0:T(2,128)(2,1)}, bf16[8,16,128]{2,1,0:T(8,128)(2,1)}) custom-call(bf16[32,16,128]{2,1,0:T(8,128)(2,1)S(1)} %all-to-all-done.gathered, bf16[384,128]{1,0:T(8,128)(2,1)S(1)} %get-tuple-element.16.first_plain, bf16[384,128]{1,0:T(8,128)(2,1)S(1)} %get-tuple-element.17.first_turned, bf16[224,256]{1,0:T(8,128)(2,1)S(1)} %get-tuple-element.18.refs_0_, ...), custom_call_target="tpu_custom_call" | custom-call | tf_op jit(solution)/shard_map/encoder/pallas_call | solution.py:407
Async XLA Ops:
  2.3 15.1 %all-to-all-start = ((bf16[32,16,128]{2,1,0:T(8,128)(2,1)}), bf16[32,16,128]{2,1,0:T(8,128)(2,1)S(1)}, u32[]{:S(2)}, u32[]{:S(2)}) async-start(bf16[32,16,128]{2,1,0:T(8,128)(2,1)} %patches.1), calls=%async_computation | async-start | bytes 262144 | tf_op jit(solution)/shard_map/all_to_all | solution.py:366

commit v9 on v8

--- a/solution.py
+++ b/solution.py
@@ -89,14 +89,11 @@
     line = lax.broadcasted_iota(jnp.int32, wide.shape, 0) // PATCH
     lane = lax.broadcasted_iota(jnp.int32, wide.shape, 1)
     wide = jnp.where(line == (lane % cells) // tile_cols, wide, 0.0)
-    blocks = [wide[:, b * cells : (b + 1) * cells] for b in range(PATCH)]
-    stacked = jnp.concatenate(blocks, axis=0).astype(jnp.bfloat16)
-    shape = (PATCH * PATCH, PATCH * height)
-    pixel = lax.broadcasted_iota(jnp.int32, shape, 0)
-    lane = lax.broadcasted_iota(jnp.int32, shape, 1)
-    mine = (lane % PATCH == pixel // PATCH) & (lane // height == pixel % PATCH)
-    mine = jnp.where(mine, 1.0, 0.0).astype(jnp.bfloat16)
-    result = jnp.dot(mine, stacked, preferred_element_type=jnp.float32).astype(jnp.bfloat16)
+    pair = 2 * PATCH
+    summed = sum(wide[at : at + pair] for at in range(pair, height, pair)) + wide[:pair]
+    summed = summed[:PATCH] + summed[PATCH:]
+    blocks = [summed[:, b * cells : (b + 1) * cells] for b in range(PATCH)]
+    result = jnp.concatenate(blocks, axis=0).astype(jnp.bfloat16)
     sent[...] = jnp.broadcast_to(result[None], sent.shape)
 
 
@@ -126,7 +123,9 @@
     pixels, width = embed_w.shape
     bias = jnp.concatenate(split(embed_b[...].reshape(1, width), 3), axis=0)
     rest = jnp.zeros((PIECE - pixels - 3, width), jnp.float32)
-    left = jnp.concatenate([embed_w[...].astype(jnp.float32), bias, rest], axis=0)
+    lines = embed_w[...].astype(jnp.float32)
+    order = [PATCH * a + b for b in range(PATCH) for a in range(PATCH)]
+    left = jnp.concatenate([lines[p : p + 1] for p in order] + [bias, rest], axis=0)
     left = (0.5 * left).astype(jnp.bfloat16)
     products = {}
     for a, b in itertools.product(range(3), range(3)):

time: 21 us -> 20.8 us (level)
  no operation moved by 1% of the time
where the time goes in v9:
time: 20.8 us; the launch traced here: 20.5 us
  starting transfers between devices  7.33 us (35%)
  Pallas kernels  6.91 us (33%)
  waiting for transfers between devices  5.58 us (27%)
  between operations  0.65 us (3%)
    all_to_all x1, starting transfers between devices, body(): gathered = lax.all_to_all(sent, ('col', 'row'), 0, 0, tiled=True)  7.33 us
    all_to_all x1, waiting for transfers between devices, body(): gathered = lax.all_to_all(sent, ('col', 'row'), 0, 0, tiled=True)  5.58 us
    pallas_call x1, Pallas kernels, body(): pl.pallas_call(functools.partial(encoder_kernel, sizes=sizes, shared=shar...  3.18 us
    pallas_call x1, Pallas kernels, body(): pl.pallas_call(functools.partial(prepare_kernel, sizes=sizes, count=len(i...  2.22 us
    pallas_call x1, Pallas kernels, body(): pl.pallas_call(functools.partial(patch_kernel, tile_rows=tile_rows, tile_...  1.51 us
  transfers between devices with their start and end apart: 1, of which 1 were waited for; matrix products, arithmetic and copies ran while one was open for 0% of the time, Pallas kernels for 11%

profile of v9, /device:TPU:0, one launch (start us, length us, event | category | flops | bytes accessed | tf_op | source)
XLA Modules:
  0.0 20.5 jit_solution(9272345684762767757)
XLA Ops:
  0.6 1.5 %patches.1 = bf16[32,16,128]{2,1,0:T(8,128)(2,1)} custom-call(f32[32,64]{1,0:T(8,128)} %tile.1), custom_call_target="tpu_custom_call" | custom-call | tf_op jit(solution)/shard_map/patches/pallas_call | solution.py:358
  2.1 7.3 %all-to-all-start = ((bf16[32,16,128]{2,1,0:T(8,128)(2,1)}), bf16[32,16,128]{2,1,0:T(8,128)(2,1)S(1)}, u32[]{:S(2)}, u32[]{:S(2)}) async-start(bf16[32,16,128]{2,1,0:T(8,128)(2,1)} %patches.1), calls=%async_computation | async-start | bytes 262144 | tf_op jit(solution)/shard_map/all_to_all | solution.py:365
  9.5 2.2 %prepare.1 = (bf16[384,128]{1,0:T(8,128)(2,1)S(1)}, bf16[384,128]{1,0:T(8,128)(2,1)S(1)}, bf16[224,256]{1,0:T(8,128)(2,1)S(1)}, bf16[112,256]{1,0:T(8,128)(2,1)S...) custom-call(bf16[16,128]{1,0:T(8,128)(2,1)} %refs_0_.1, ...), custom_call_target="tpu_custom_call" | custom-call | tf_op jit(solution)/shard_map/prepare/pallas_call | solution.py:380
  11.7 5.6 %all-to-all-done.gathered = bf16[32,16,128]{2,1,0:T(8,128)(2,1)S(1)} async-done(((bf16[32,16,128]{2,1,0:T(8,128)(2,1)}), bf16[32,16,128]{2,1,0:T(8,128)(2,1)S(1)}, u32[]{:S(2)}, u32[]{:S(2)}) %all-to-all-start) | async-done | bytes 131104 | tf_op jit(solution)/shard_map/all_to_all | solution.py:365
  17.3 3.2 %encoder.1 = (bf16[2,256]{1,0:T(2,128)(2,1)}, bf16[8,16,128]{2,1,0:T(8,128)(2,1)}) custom-call(bf16[32,16,128]{2,1,0:T(8,128)(2,1)S(1)} %all-to-all-done.gathered, bf16[384,128]{1,0:T(8,128)(2,1)S(1)} %get-tuple-element.16.first_plain, bf16[384,128]{1,0:T(8,128)(2,1)S(1)} %get-tuple-element.17.first_turned, bf16[224,256]{1,0:T(8,128)(2,1)S(1)} %get-tuple-element.18.refs_0_, ...), custom_call_target="tpu_custom_call" | custom-call | tf_op jit(solution)/shard_map/encoder/pallas_call | solution.py:406
Async XLA Ops:
  2.1 15.1 %all-to-all-start = ((bf16[32,16,128]{2,1,0:T(8,128)(2,1)}), bf16[32,16,128]{2,1,0:T(8,128)(2,1)S(1)}, u32[]{:S(2)}, u32[]{:S(2)}) async-start(bf16[32,16,128]{2,1,0:T(8,128)(2,1)} %patches.1), calls=%async_computation | async-start | bytes 262144 | tf_op jit(solution)/shard_map/all_to_all | solution.py:365

commit v10 on v9

--- a/solution.py
+++ b/solution.py
@@ -197,9 +197,10 @@
         count = value.shape[0]
         base = 0 if shared else start
         stage[pl.ds(base, count), PAD : PAD + span, :] = value
-        return [
-            stage[pl.ds(base, count), PAD - 1 + at : PAD - 1 + at + span, :] for at in range(3)
+        before, after = [
+            stage[pl.ds(base, count), PAD + at : PAD + at + span, :] for at in (-1, 1)
         ]
+        return [before, value, after]
 
     def emit(pair, start, value):
         target, stage = pair

time: 20.8 us -> 20.8 us (level)
  no operation moved by 1% of the time
where the time goes in v10:
time: 20.8 us; the launch traced here: 20.4 us
  starting transfers between devices  7.33 us (35%)
  Pallas kernels  6.87 us (33%)
  waiting for transfers between devices  5.58 us (27%)
  between operations  0.65 us (3%)
    all_to_all x1, starting transfers between devices, body(): gathered = lax.all_to_all(sent, ('col', 'row'), 0, 0, tiled=True)  7.33 us
    all_to_all x1, waiting for transfers between devices, body(): gathered = lax.all_to_all(sent, ('col', 'row'), 0, 0, tiled=True)  5.58 us
    pallas_call x1, Pallas kernels, body(): pl.pallas_call(functools.partial(encoder_kernel, sizes=sizes, shared=shar...  3.13 us
    pallas_call x1, Pallas kernels, body(): pl.pallas_call(functools.partial(prepare_kernel, sizes=sizes, count=len(i...  2.22 us
    pallas_call x1, Pallas kernels, body(): pl.pallas_call(functools.partial(patch_kernel, tile_rows=tile_rows, tile_...  1.51 us
  transfers between devices with their start and end apart: 1, of which 1 were waited for; matrix products, arithmetic and copies ran while one was open for 0% of the time, Pallas kernels for 11%

profile of v10, /device:TPU:0, one launch (start us, length us, event | category | flops | bytes accessed | tf_op | source)
XLA Modules:
  0.0 20.4 jit_solution(12428921563460363255)
XLA Ops:
  0.6 1.5 %patches.1 = bf16[32,16,128]{2,1,0:T(8,128)(2,1)} custom-call(f32[32,64]{1,0:T(8,128)} %tile.1), custom_call_target="tpu_custom_call" | custom-call | tf_op jit(solution)/shard_map/patches/pallas_call | solution.py:359
  2.1 7.3 %all-to-all-start = ((bf16[32,16,128]{2,1,0:T(8,128)(2,1)}), bf16[32,16,128]{2,1,0:T(8,128)(2,1)S(1)}, u32[]{:S(2)}, u32[]{:S(2)}) async-start(bf16[32,16,128]{2,1,0:T(8,128)(2,1)} %patches.1), calls=%async_computation | async-start | bytes 262144 | tf_op jit(solution)/shard_map/all_to_all | solution.py:366
  9.5 2.2 %prepare.1 = (bf16[384,128]{1,0:T(8,128)(2,1)S(1)}, bf16[384,128]{1,0:T(8,128)(2,1)S(1)}, bf16[224,256]{1,0:T(8,128)(2,1)S(1)}, bf16[112,256]{1,0:T(8,128)(2,1)S...) custom-call(bf16[16,128]{1,0:T(8,128)(2,1)} %refs_0_.1, ...), custom_call_target="tpu_custom_call" | custom-call | tf_op jit(solution)/shard_map/prepare/pallas_call | solution.py:381
  11.7 5.6 %all-to-all-done.gathered = bf16[32,16,128]{2,1,0:T(8,128)(2,1)S(1)} async-done(((bf16[32,16,128]{2,1,0:T(8,128)(2,1)}), bf16[32,16,128]{2,1,0:T(8,128)(2,1)S(1)}, u32[]{:S(2)}, u32[]{:S(2)}) %all-to-all-start) | async-done | bytes 131104 | tf_op jit(solution)/shard_map/all_to_all | solution.py:366
  17.3 3.1 %encoder.1 = (bf16[2,256]{1,0:T(2,128)(2,1)}, bf16[8,16,128]{2,1,0:T(8,128)(2,1)}) custom-call(bf16[32,16,128]{2,1,0:T(8,128)(2,1)S(1)} %all-to-all-done.gathered, bf16[384,128]{1,0:T(8,128)(2,1)S(1)} %get-tuple-element.16.first_plain, bf16[384,128]{1,0:T(8,128)(2,1)S(1)} %get-tuple-element.17.first_turned, bf16[224,256]{1,0:T(8,128)(2,1)S(1)} %get-tuple-element.18.refs_0_, ...), custom_call_target="tpu_custom_call" | custom-call | tf_op jit(solution)/shard_map/encoder/pallas_call | solution.py:407
Async XLA Ops:
  2.1 15.1 %all-to-all-start = ((bf16[32,16,128]{2,1,0:T(8,128)(2,1)}), bf16[32,16,128]{2,1,0:T(8,128)(2,1)S(1)}, u32[]{:S(2)}, u32[]{:S(2)}) async-start(bf16[32,16,128]{2,1,0:T(8,128)(2,1)} %patches.1), calls=%async_computation | async-start | bytes 262144 | tf_op jit(solution)/shard_map/all_to_all | solution.py:366
